TPU v7x, 256 devices: a whole 4x4x8 slice. The times are simulated.
256 devices in a mesh: lon: 32 (over x_lo, z, core), lat: 8 (over y, x_hi).
Axes of the slice: x: 4 (x_hi: 2, x_lo: 2; x = x_hi * 2 + x_lo), y: 4, z: 8, core: 2. Of those that a mesh axis runs over, the one named last changes fastest.
Arguments:
- heat_anomaly: float32 [16, 256, 4096], P(None, 'lat', 'lon'), may hold values from -11 to 11
- saltiness_anomaly: float32 [16, 256, 4096], P(None, 'lat', 'lon'), may hold values from -3 to 3
- zonal_stability_ratio: float32 [16, 256, 4096], P(None, 'lat', 'lon'), may hold values from -0.4 to 0.4
- meridional_stability_ratio: float32 [16, 256, 4096], P(None, 'lat', 'lon'), may hold values from -0.4 to 0.4
- ocean_layer_count: int32 [256, 4096], P('lat', 'lon'), may hold values from 0 to 16
Outputs:
- temperature_next: float32 [16, 256, 4096], P(None, 'lat', 'lon')
- salinity_next: float32 [16, 256, 4096], P(None, 'lat', 'lon')
All inputs are finite; a program needn't handle non-finite values.
Results may differ from a plain program's by a relative error of at most 0.0003.
Values sent between devices are 32-bit elements; how exact they have to be, the bound alone decides.
A program may use at most 64 MiB of HBM per device.

v0:
```python
import jax
import jax.numpy as jnp
from jax import lax
from jax.sharding import PartitionSpec as P

heat_swelling_alpha = 0.1655
coef_beta = 0.76554
cabbeling_parameter = 0.05952
lambda_salt = 0.00054914
thermobaric_parameter = 0.0001497
press_salt = 1.109e-05
cross_coupling_contribution = 0.0024341
total_depth = 5000.0
kappa_iso = 0.1
slope_max = 1.0
strat_min = 0.1


def extended(array, sides, width, wrap):
    for axis, dim in sides:
        devices, length = (lax.axis_size(axis), array.shape[dim])
        up = [(i, (i + 1) % devices) for i in range(devices if wrap else devices - 1)]
        down = [(j, i) for i, j in up]
        last = lax.slice_in_dim(array, length - width, length, axis=dim)
        first = lax.slice_in_dim(array, 0, width, axis=dim)
        before = lax.ppermute(last, axis, up)
        after = lax.ppermute(first, axis, down)
        array = jnp.concatenate([before, array, after], axis=dim)
    return array


def passed_along(array, axis, by):
    devices = lax.axis_size(axis)
    return lax.ppermute(array, axis, [(i, (i + by) % devices) for i in range(devices)])


def passed_along_2(array, axis, by):
    devices = lax.axis_size(axis)
    pairs = [(i, i + by) for i in range(devices) if 0 <= i + by < devices]
    return lax.ppermute(array, axis, pairs)


def minmod(former, second):
    return jnp.where(
        former * second > 0.0, jnp.sign(former) * jnp.minimum(jnp.abs(former), jnp.abs(second)), 0.0
    )


def seawater_heaviness(heat_anomaly, saltiness_anomaly, seafloor_distances):
    return (
        -heat_swelling_alpha
        * (
            1.0
            + 0.5 * cabbeling_parameter * heat_anomaly
            + thermobaric_parameter * seafloor_distances
        )
        * heat_anomaly
        + coef_beta
        * (1.0 - 0.5 * lambda_salt * saltiness_anomaly - press_salt * seafloor_distances)
        * saltiness_anomaly
        - cross_coupling_contribution * heat_anomaly * saltiness_anomaly
    )


def vertical_diff(field):
    along = field.ndim - 3
    layer_stack_sum = field.shape[along]
    top_part = lax.slice_in_dim(field, 1, 2, axis=along) - lax.slice_in_dim(field, 0, 1, axis=along)
    middle = 0.5 * (
        lax.slice_in_dim(field, 2, layer_stack_sum, axis=along)
        - lax.slice_in_dim(field, 0, layer_stack_sum - 2, axis=along)
    )
    bottom = lax.slice_in_dim(
        field, layer_stack_sum - 1, layer_stack_sum, axis=along
    ) - lax.slice_in_dim(field, layer_stack_sum - 2, layer_stack_sum - 1, axis=along)
    return jnp.concatenate([top_part, middle, bottom], axis=along)


def face_flux(tracers, tracer_vert, rho_field, rho_vert, ocean_presence_flags, face_speed, along):

    def window(array, lower, upper):
        axis_pos = array.ndim + along
        return lax.slice_in_dim(array, lower, array.shape[axis_pos] - upper, axis=axis_pos)

    wet_face = window(ocean_presence_flags, 0, 1) * window(ocean_presence_flags, 1, 0)
    masked_step = wet_face * (window(tracers, 1, 0) - window(tracers, 0, 1))
    step_back = window(masked_step, 0, 2)
    step_here = window(masked_step, 1, 1)
    step_ahead = window(masked_step, 2, 0)
    cell_left = window(tracers, 1, 2)
    cell_right = window(tracers, 2, 1)
    face_wet = window(wet_face, 1, 1)
    positive = jnp.maximum(face_speed, 0.0)
    negative = jnp.minimum(face_speed, 0.0)
    advective = face_wet * (
        positive * (cell_left + 0.5 * (1.0 - face_speed) * minmod(step_back, step_here))
        + negative * (cell_right - 0.5 * (1.0 + face_speed) * minmod(step_ahead, step_here))
    )
    rho_step = window(rho_field, 2, 1) - window(rho_field, 1, 2)
    strat_face = jnp.maximum(0.5 * (window(rho_vert, 1, 2) + window(rho_vert, 2, 1)), strat_min)
    slope_face = jnp.clip(-rho_step / strat_face, -slope_max, slope_max)
    vert_face = 0.5 * (window(tracer_vert, 1, 2) + window(tracer_vert, 2, 1))
    isoneutral = -kappa_iso * face_wet * (cell_right - cell_left + slope_face * vert_face)
    flux_total = advective + isoneutral
    return window(flux_total, 0, 1) - window(flux_total, 1, 0)


def stencil(padded, east_cols, north_rows):
    layer_stack_sum = padded.shape[1]
    depth_levels = (
        total_depth
        * (lax.broadcasted_iota(jnp.float32, (layer_stack_sum, 1, 1), 0) + 0.5)
        / layer_stack_sum
    )
    tracers = padded[:2]
    ocean_presence_flags = padded[2]
    rho_field = seawater_heaviness(padded[0], padded[1], depth_levels)
    rho_vert = vertical_diff(rho_field)
    tracer_vert = vertical_diff(tracers)
    along_x = face_flux(
        tracers[:, :, 2:-2, :],
        tracer_vert[:, :, 2:-2, :],
        rho_field[:, 2:-2, :],
        rho_vert[:, 2:-2, :],
        ocean_presence_flags[:, 2:-2, :],
        east_cols,
        -1,
    )
    along_y = face_flux(
        tracers[:, :, :, 2:-2],
        tracer_vert[:, :, :, 2:-2],
        rho_field[:, :, 2:-2],
        rho_vert[:, :, 2:-2],
        ocean_presence_flags[:, :, 2:-2],
        north_rows,
        -2,
    )
    interior = tracers[:, :, 2:-2, 2:-2]
    return ocean_presence_flags[:, 2:-2, 2:-2] * (interior + along_x + along_y)


def body(
    heat_anomaly,
    saltiness_anomaly,
    zonal_stability_ratio,
    meridional_stability_ratio,
    ocean_layer_count,
):
    layer_stack_sum, latitude_band_sum, profile_sum = heat_anomaly.shape
    ocean_presence_flags = (
        lax.broadcasted_iota(jnp.int32, (layer_stack_sum, 1, 1), 0) < ocean_layer_count[None]
    ).astype(jnp.float32)
    scalar_quantities = jnp.stack([heat_anomaly, saltiness_anomaly, ocean_presence_flags])
    lon_padded = extended(scalar_quantities, (("lon", 3),), 2, True)
    padded = extended(lon_padded, (("lat", 2),), 2, False)
    whole_rows = lax.all_gather(
        scalar_quantities[:3, :, latitude_band_sum - 3 :, :], "lon", axis=3, tiled=True
    )
    flipped = jnp.flip(whole_rows, -1)
    offset = lax.axis_index("lon") * profile_sum
    rolled = jnp.concatenate([flipped[..., -1:], flipped], axis=-1)
    next_rows = lax.dynamic_slice_in_dim(rolled, offset, profile_sum, 3)
    ghost_rows = jnp.flip(next_rows[:, :, 0:2, :], 2)
    top_device = lax.axis_index("lat") == lax.axis_size("lat") - 1
    current = padded[:3, :, latitude_band_sum + 2 :, 2 : profile_sum + 2]
    padded = padded.at[:3, :, latitude_band_sum + 2 :, 2 : profile_sum + 2].set(
        jnp.where(top_device, ghost_rows, current)
    )
    west_column = passed_along(zonal_stability_ratio[:, :, profile_sum - 1], "lon", 1)
    east_cols = jnp.concatenate([west_column[:, :, None], zonal_stability_ratio], axis=2)
    south_row = passed_along_2(meridional_stability_ratio[:, latitude_band_sum - 1, :], "lat", 1)
    north_rows = jnp.concatenate([south_row[:, None, :], meridional_stability_ratio], axis=1)
    result = stencil(padded, east_cols, north_rows)
    return (result[0], result[1])


def solution(mesh):
    in_specs = (
        P(None, "lat", "lon"),
        P(None, "lat", "lon"),
        P(None, "lat", "lon"),
        P(None, "lat", "lon"),
        P("lat", "lon"),
    )
    out_specs = (P(None, "lat", "lon"), P(None, "lat", "lon"))
    return jax.shard_map(body, mesh=mesh, in_specs=in_specs, out_specs=out_specs, check_vma=False)
```

profile of v0, /device:TPU:28, one launch (start us, length us, event | category | flops | bytes accessed | tf_op | source)
XLA Modules:
  0.0 123.5 jit_solution(3798697741980197287)
XLA Ops:
  7.2 0.0 all-gather.2.cloned.1.call-start
  7.2 0.7 fusion.27
  8.0 1.1 pad_maximum_fusion.2
  9.0 0.7 slice.340
  9.7 0.0 all-gather.2.cloned.1.call-update
  9.7 0.3 fusion.31
  10.1 0.3 copy.82
  10.4 6.0 %collective-permute-start.1 = (f32[3,16,32,2]{2,1,3,0:T(8,128)S(1)}, f32[3,16,32,2]{2,1,3,0:T(8,128)S(1)}, u32[]{:S(2)}, u32[]{:S(2)}) collective-permute-start(f32[3,16,32,2]{2,1,3,0:T(8,128)S(1)} %copy.82), channel_id=1, source_target_pairs={{8,0},{16,8},{24,16},{32,24},{40,32},{48,40},{56,48},{64,56},{72,6... | collective-permute-start | bytes 36872 | tf_op jit(solution)/shard_map/ppermute | solution.py:27
  16.4 0.3 copy.81
  16.7 0.1 collective-permute-start
  16.8 0.2 copy.77
  17.0 1.3 %collective-permute-start.5 = (f32[16,128]{1,0:T(8,128)S(1)}, f32[16,128]{1,0:T(8,128)S(1)}, u32[]{:S(2)}, u32[]{:S(2)}) collective-permute-start(f32[16,128]{1,0:T(8,128)S(1)} %slice_bitcast_fusion.5), channel_id=1, source_target_pairs={{0,1},{1,2},{2,3},{3,4},{4,5},{5,6},{6,7},{8,9},{9,10},{10,11},{11... | collective-permute-start | bytes 24584 | tf_op jit(solution)/shard_map/ppermute | solution.py:40
  18.3 0.1 slice.287
  18.4 0.2 copy.83
  18.6 0.1 collective-permute-start.4
  18.7 0.5 copy.70
  19.2 0.2 copy.76
  19.3 4.5 %collective-permute-done.4 = f32[16,32]{1,0:T(8,128)S(1)} collective-permute-done((f32[16,32]{1,0:T(8,128)S(1)}, f32[16,32]{1,0:T(8,128)S(1)}, u32[]{:S(2)}, u32[]{:S(2)}) %collective-permute-start.4) | collective-permute-done | bytes 2080 | tf_op jit(solution)/shard_map/ppermute | solution.py:34
  23.8 0.2 copy.75
  24.0 1.7 %broadcast_maximum_fusion = (f32[16,32,129]{2,0,1:T(8,128)}, f32[16,32,129]{2,0,1:T(8,128)}, f32[16,32,129]{2,0,1:T(8,128)}, f32[16,32,129]{2,0,1:T(8,128)}) fusion(f32[16,32,128]{2,0,1:T(8,128)S(1)} %copy.76, f32[16,32,1]{2,0,1:T(8,128)S(1)} %copy.75), kind=kLoop, calls=%fused_computation.65 | loop fusion | flops 462336 | bytes 1320960 | tf_op jit(solution)/shard_map/max | solution.py:93
  25.8 0.4 copy.71
  26.2 0.4 copy.69
  26.7 0.1 pad_maximum_fusion.8
  26.8 6.2 %collective-permute-start.3 = (f32[3,16,2,132]{3,1,2,0:T(8,128)S(1)}, f32[3,16,2,132]{3,1,2,0:T(8,128)S(1)}, u32[]{:S(2)}, u32[]{:S(2)}) collective-permute-start(f32[3,16,2,132]{3,1,2,0:T(8,128)S(1)} %get-tuple-element.23), channel_id=1, source_target_pairs={{1,0},{2,1},{3,2},{4,3},{5,4},{6,5},{7,6},{9,8},{10,9},{11,10},{12... | collective-permute-start | bytes 152072 | tf_op jit(solution)/shard_map/ppermute | solution.py:27
  33.0 1.5 %collective-permute-start.2 = (f32[3,16,2,132]{3,1,2,0:T(8,128)S(1)}, f32[3,16,2,132]{3,1,2,0:T(8,128)S(1)}, u32[]{:S(2)}, u32[]{:S(2)}) collective-permute-start(f32[3,16,2,132]{3,1,2,0:T(8,128)S(1)} %get-tuple-element.22), channel_id=1, source_target_pairs={{0,1},{1,2},{2,3},{3,4},{4,5},{5,6},{6,7},{8,9},{9,10},{10,11},{11... | collective-permute-start | bytes 152072 | tf_op jit(solution)/shard_map/ppermute | solution.py:26
  34.5 1.1 broadcast_maximum_fusion.1
  35.6 0.1 collective-permute-done.3
  35.7 5.9 %collective-permute-done.2 = f32[3,16,2,132]{3,1,2,0:T(8,128)S(1)} collective-permute-done((f32[3,16,2,132]{3,1,2,0:T(8,128)S(1)}, f32[3,16,2,132]{3,1,2,0:T(8,128)S(1)}, u32[]{:S(2)}, u32[]{:S(2)}) %collective-permute-start.2) | collective-permute-done | bytes 50720 | tf_op jit(solution)/shard_map/ppermute | solution.py:26
  41.5 1.8 %pad_maximum_fusion = f32[3,16,36,132]{3,1,2,0:T(8,128)S(1)} fusion(f32[3,16,2,132]{3,1,2,0:T(8,128)S(1)} %collective-permute-done.3, f32[3,16,32,2]{3,1,2,0:T(8,128)S(1)} %copy.71, f32[3,16,32,128]{3,1,2,0:T(8,128)S(1)} %copy.70, f32[3,16,32,2]{3,1,2,0:T(8,128)} %copy-done, f32[3,16,2,132]{3,1,2,0:T(8,128)S(1)} %collective-permute-done.2), kind=kLoop, calls=%fused_computation.2 | loop fusion | flops 912384 | bytes 1824768 | tf_op jit(solution)/shard_map/concatenate | solution.py:28
  43.4 38.6 %all-gather.2.cloned.1.call-done = f32[3,16,3,4096]{3,2,1,0:T(4,128)} async-done(((f32[3,16,3,128]{3,2,1,0:T(4,128)}), f32[3,16,3,4096]{3,2,1,0:T(4,128)}) %all-gather.2.cloned.1.call-update) | async-done | bytes 2359312 | tf_op jit(solution)/shard_map/all_gather | solution.py:156
  81.9 0.9 slice.341
  82.9 19.4 %rev.8 = f32[3,16,3,4096]{3,2,1,0:T(4,128)} reverse(f32[3,16,3,4096]{3,2,1,0:T(4,128)} %all-gather.2.cloned.1.call-done), dimensions={3} | reverse | bytes 4718592 | tf_op jit(solution)/shard_map/jit(_flip)/rev | solution.py:159
  102.2 3.3 %copy.73 = f32[3,16,3,4096]{3,1,2,0:T(8,128)S(1)} copy(f32[3,16,3,4096]{3,2,1,0:T(4,128)} %rev.8) | data formatting | bytes 4718592 | tf_op jit(solution)/shard_map/jit(_flip)/rev | solution.py:159
  105.5 0.1 fusion.28
  105.6 0.1 slice_select_fusion
  105.7 1.1 scatter.4
  106.8 0.2 slice_subtract_fusion.9
  107.0 0.2 fusion
  107.2 0.3 multiply_subtract_fusion
  107.5 0.1 slice_subtract_fusion.11
  107.6 0.1 fusion.6
  107.7 0.2 slice_multiply_fusion.1
  107.9 0.4 fusion.7
  108.3 0.2 slice_multiply_fusion
  108.5 0.1 pad_maximum_fusion.3
  108.7 0.4 fusion.25
  109.0 0.6 fusion.19
  109.7 0.3 fusion.5
  110.0 0.2 fusion.32
  110.2 0.1 slice.344
  110.4 0.3 pad_maximum_fusion.1
  110.7 0.5 copy-done.5
  111.2 0.1 copy-done.6
  111.2 0.1 copy-done.7
  111.3 0.1 copy-done.8
  111.4 0.7 fusion.11
  112.1 0.3 copy-done.1
  112.5 0.2 copy-done.2
  112.6 0.2 copy-done.3
  112.8 0.2 copy-done.4
  112.9 1.7 %fusion.4 = f32[2,16,32,129]{3,1,2,0:T(8,128)S(1)} fusion(f32[2,16,36,132]{3,1,2,0:T(8,128)S(1)} %pad_maximum_fusion.1, f32[3,16,36,132]{3,1,2,0:T(8,128)S(1)} %scatter.4, f32[2,16,32,131]{3,1,2,0:T(8,128)S(1)} %fusion.5, f32[16,32,129]{2,0,1:T(8,128)S(1)} %fusion.19, f32[16,32,129]{2,0,1:T(8,128)S(1)} %get-tuple-element.33, ...), kind=kLoop, calls=%fused_computation.10 | loop fusion | flops 3830784 | bytes 6076416 | tf_op jit(solution)/shard_map/add | solution.py:104
  114.6 0.4 fusion.13
  115.1 0.8 copy.79
  115.8 0.8 copy.80
  (23 shorter events, 0.2 us)
Async XLA Ops:
  7.2 74.8 %all-gather.2.cloned.1.call-start = ((), (), s32[]{:S(2)}) async-start(), calls=%async_computation | async-start | bytes 3244032 | tf_op jit(solution)/shard_map/all_gather | solution.py:156
  9.7 7.1 %copy-start.10 = (f32[16,32,128]{2,1,0:T(8,128)S(1)}, f32[16,32,128]{2,1,0:T(8,128)}, u32[]{:S(2)}) copy-start(f32[16,32,128]{2,1,0:T(8,128)} %param.10) | copy-start | bytes 786436
  10.0 8.3 %copy-start.9 = (f32[16,32,128]{2,1,0:T(8,128)S(1)}, f32[16,32,128]{2,1,0:T(8,128)}, u32[]{:S(2)}) copy-start(f32[16,32,128]{2,1,0:T(8,128)} %param.9) | copy-start | bytes 786436
  10.4 15.4 %collective-permute-start.1 = (f32[3,16,32,2]{2,1,3,0:T(8,128)S(1)}, f32[3,16,32,2]{2,1,3,0:T(8,128)S(1)}, u32[]{:S(2)}, u32[]{:S(2)}) collective-permute-start(f32[3,16,32,2]{2,1,3,0:T(8,128)S(1)} %copy.82), channel_id=1, source_target_pairs={{8,0},{16,8},{24,16},{32,24},{40,32},{48,40},{56,48},{64,56},{72,6... | collective-permute-start | bytes 36872 | tf_op jit(solution)/shard_map/ppermute | solution.py:27
  16.7 9.5 %collective-permute-start = (f32[3,16,32,2]{2,1,3,0:T(8,128)S(1)}, f32[3,16,32,2]{2,1,3,0:T(8,128)S(1)}, u32[]{:S(2)}, u32[]{:S(2)}) collective-permute-start(f32[3,16,32,2]{2,1,3,0:T(8,128)S(1)} %copy.81), channel_id=1, source_target_pairs={{0,8},{8,16},{16,24},{24,32},{32,40},{40,48},{48,56},{56,64},{64,7... | collective-permute-start | bytes 36872 | tf_op jit(solution)/shard_map/ppermute | solution.py:26
  17.0 17.5 %collective-permute-start.5 = (f32[16,128]{1,0:T(8,128)S(1)}, f32[16,128]{1,0:T(8,128)S(1)}, u32[]{:S(2)}, u32[]{:S(2)}) collective-permute-start(f32[16,128]{1,0:T(8,128)S(1)} %slice_bitcast_fusion.5), channel_id=1, source_target_pairs={{0,1},{1,2},{2,3},{3,4},{4,5},{5,6},{6,7},{8,9},{9,10},{10,11},{11... | collective-permute-start | bytes 24584 | tf_op jit(solution)/shard_map/ppermute | solution.py:40
  18.6 5.2 %collective-permute-start.4 = (f32[16,32]{1,0:T(8,128)S(1)}, f32[16,32]{1,0:T(8,128)S(1)}, u32[]{:S(2)}, u32[]{:S(2)}) collective-permute-start(f32[16,32]{1,0:T(8,128)S(1)} %bitcast.24), channel_id=1, source_target_pairs={{0,8},{8,16},{16,24},{24,32},{32,40},{40,48},{48,56},{56,64},{64,7... | collective-permute-start | bytes 6152 | tf_op jit(solution)/shard_map/ppermute | solution.py:34
  26.7 8.9 %copy-start = (f32[3,16,32,2]{3,1,2,0:T(8,128)}, f32[3,16,32,2]{3,1,2,0:T(8,128)S(1)}, u32[]{:S(2)}) copy-start(f32[3,16,32,2]{3,1,2,0:T(8,128)S(1)} %copy.69) | copy-start | bytes 36868
  26.8 8.8 %collective-permute-start.3 = (f32[3,16,2,132]{3,1,2,0:T(8,128)S(1)}, f32[3,16,2,132]{3,1,2,0:T(8,128)S(1)}, u32[]{:S(2)}, u32[]{:S(2)}) collective-permute-start(f32[3,16,2,132]{3,1,2,0:T(8,128)S(1)} %get-tuple-element.23), channel_id=1, source_target_pairs={{1,0},{2,1},{3,2},{4,3},{5,4},{6,5},{7,6},{9,8},{10,9},{11,10},{12... | collective-permute-start | bytes 152072 | tf_op jit(solution)/shard_map/ppermute | solution.py:27
  33.0 8.5 %collective-permute-start.2 = (f32[3,16,2,132]{3,1,2,0:T(8,128)S(1)}, f32[3,16,2,132]{3,1,2,0:T(8,128)S(1)}, u32[]{:S(2)}, u32[]{:S(2)}) collective-permute-start(f32[3,16,2,132]{3,1,2,0:T(8,128)S(1)} %get-tuple-element.22), channel_id=1, source_target_pairs={{0,1},{1,2},{2,3},{3,4},{4,5},{5,6},{6,7},{8,9},{9,10},{10,11},{11... | collective-permute-start | bytes 152072 | tf_op jit(solution)/shard_map/ppermute | solution.py:26
  110.2 1.0 copy-start.5
  110.2 1.0 copy-start.6
  110.2 1.1 copy-start.7
  110.2 1.2 copy-start.8
  111.4 1.0 copy-start.1
  111.4 1.2 copy-start.2
  111.4 1.4 %copy-start.3 = (f32[16,32,129]{2,0,1:T(8,128)S(1)}, f32[16,32,129]{2,0,1:T(8,128)}, u32[]{:S(2)}) copy-start(f32[16,32,129]{2,0,1:T(8,128)} %get-tuple-element.36) | copy-start | bytes 792580
  111.4 1.5 %copy-start.4 = (f32[16,32,129]{2,0,1:T(8,128)S(1)}, f32[16,32,129]{2,0,1:T(8,128)}, u32[]{:S(2)}) copy-start(f32[16,32,129]{2,0,1:T(8,128)} %get-tuple-element.37) | copy-start | bytes 792580
Sparse Core Ops, SparseCore 0:
  10.3 71.5 all-gather.1
where the time goes:
time: 126 us; the launch traced here: 123 us
  waiting for transfers between devices  49 us (39%)
  local copies, waits for them, and re-layouts  31.8 us (25%)
  starting transfers between devices  15.1 us (12%)
  between operations  14.4 us (11%)
  other arithmetic  13.1 us (10%)
    all_gather x1, waiting for transfers between devices, body(): lax.all_gather(scalar_quantities[:3, :, latitude_band_sum - 3:, :], 'lon'...  38.6 us
    rev x2, local copies, waits for them, and re-layouts, body(): flipped = jnp.flip(whole_rows, -1)  22.7 us
    ppermute x2, starting transfers between devices, extended(): after = lax.ppermute(first, axis, down)  12.1 us
    ppermute x2, waiting for transfers between devices, extended(): before = lax.ppermute(last, axis, up)  5.88 us
    ppermute x1, waiting for transfers between devices, passed_along(): lax.ppermute(array, axis, [(i, (i + by) % devices) for i in range(devices)])  4.52 us
    unnamed x29, local copies, waits for them, and re-layouts  4.33 us
    max x2, other arithmetic, face_flux(): positive = jnp.maximum(face_speed, 0.0)  2.84 us
  transfers between devices with their start and end apart: 7, of which 4 were waited for; matrix products, arithmetic and copies ran while one was open for 6% of the time, Pallas kernels for 0%

commit v1 on v0

v1 whole, which is shorter than its diff:
```python
import jax
import jax.numpy as jnp
from jax import lax
from jax.experimental import pallas as pl
from jax.experimental.pallas import tpu as pltpu
from jax.sharding import PartitionSpec as P

ALPHA = 0.1655
BETA = 0.76554
CABBELING = 0.05952
LAMBDA_SALT = 0.00054914
THERMOBARIC = 0.0001497
PRESS_SALT = 1.109e-05
CROSS = 0.0024341
TOTAL_DEPTH = 5000.0
KAPPA = 0.1
SLOPE_MAX = 1.0
STRAT_MIN = 0.1

MESH = pl.DeviceIdType.MESH
F32 = jnp.float32
I32 = jnp.int32

PAD = 8
SLOT = 8
MID = 3


def density(t, s, z):
    lead = -ALPHA - (ALPHA * THERMOBARIC) * z
    salt = BETA - (BETA * PRESS_SALT) * z
    return t * (lead + (-0.5 * ALPHA * CABBELING) * t - CROSS * s) + s * (salt - (0.5 * BETA * LAMBDA_SALT) * s)


def slope_term(rho_diff, rho_zsum, half_scale):
    strat = jnp.maximum(half_scale * rho_zsum, STRAT_MIN)
    slope = jnp.clip(-rho_diff / strat, -SLOPE_MAX, SLOPE_MAX)
    return slope * (KAPPA * half_scale)


def courant_terms(c):
    up = c > 0.0
    coef = jnp.where(up, 0.5, -0.5) - 0.5 * c
    return up, coef


def tracer_flux(face, c, up, coef, sk, qa, qb, d, back, ahead, zsum):
    step = jnp.where(up, back, ahead)
    limited = jnp.minimum(jnp.maximum(step, jnp.minimum(d, 0.0)), jnp.maximum(d, 0.0))
    adv = c * (jnp.where(up, qa, qb) + coef * limited)
    return jnp.where(face, adv - (KAPPA * d + sk * zsum), 0.0)


def lanes(x, shift):
    return pltpu.roll(x, shift % 128, axis=x.ndim - 1)


def rows_by(x, shift):
    return pltpu.roll(x, shift % 8, axis=x.ndim - 2)


def make_kernel(nlon, nlat, levels, rows):
    groups = rows // 8
    per = 16 // groups
    packs = levels // per
    span = SLOT * groups
    top_row = PAD + rows

    def depth(k):
        return TOTAL_DEPTH * (k + 0.5) / levels

    def kernel(
        t_hbm, s_hbm, u_hbm, v_hbm, n_hbm, t_out, s_out,
        q, rho, u, v, n, face_x, keep_x, face_y, keep_y, fy,
        px, from_w, from_e, h, hv, hn, fa, fb, fan, fbn, ex, ey,
        load_sem, send_sem, recv_sem,
    ):
        lon = lax.axis_index("lon")
        lat = lax.axis_index("lat")
        east = lax.rem(lon + 1, nlon)
        west = lax.rem(lon + nlon - 1, nlon)
        has_south = lat > 0
        has_north = lat < nlat - 1
        top = lat == nlat - 1
        mirror = nlon - 1 - lon
        mirror_next = lax.rem(nlon - lon, nlon)
        mirror_far = mirror_next != lon
        top_far = jnp.logical_and(top, mirror_far)
        top_self = jnp.logical_and(top, jnp.logical_not(mirror_far))

        barrier = pltpu.get_barrier_semaphore()

        def greet(device):
            pl.semaphore_signal(barrier, inc=1, device_id=device, device_id_type=MESH)

        @pl.when(has_south)
        def _():
            greet({"lat": lat - 1})

        @pl.when(has_north)
        def _():
            greet({"lat": lat + 1})

        @pl.when(top)
        def _():
            greet({"lon": mirror})

        @pl.when(top_far)
        def _():
            greet({"lon": mirror_next})

        greet({"lon": east})
        greet({"lon": west})

        body_rows = pl.ds(PAD, rows)
        loads = [
            pltpu.make_async_copy(n_hbm, n.at[body_rows], load_sem.at[0]),
            pltpu.make_async_copy(t_hbm, q.at[0, :, body_rows], load_sem.at[1]),
            pltpu.make_async_copy(s_hbm, q.at[1, :, body_rows], load_sem.at[2]),
            pltpu.make_async_copy(u_hbm, u, load_sem.at[3]),
            pltpu.make_async_copy(v_hbm, v.at[:, body_rows], load_sem.at[4]),
        ]
        for load in loads:
            load.start()

        lane = lax.broadcasted_iota(I32, (8, 128), 1)
        row = lax.broadcasted_iota(I32, (8, 128), 0)
        slot_of = lane // SLOT
        sl = lane % SLOT

        loads[0].wait()
        packed_n = jnp.zeros((8, 128), F32)
        for slot in range(16):
            part = n[pl.ds(PAD + 8 * (slot % groups), 8)].astype(F32)
            packed_n = jnp.where(slot_of == slot, lanes(part, SLOT * slot + MID), packed_n)
        px[2 * packs] = packed_n
        loads[1].wait()
        loads[2].wait()
        loads[3].wait()

        @pl.loop(0, packs)
        def _(m):
            for field in range(3):
                packed = jnp.zeros((8, 128), F32)
                for slot in range(16):
                    k = packs * (slot // groups) + m
                    g = slot % groups
                    if field < 2:
                        part = q[field, k, pl.ds(PAD + 8 * g, 8)]
                    else:
                        part = u[k, pl.ds(8 * g, 8)]
                    packed = jnp.where(slot_of == slot, lanes(part, SLOT * slot + MID), packed)
                px[(0, packs, 2 * packs + 1)[field] + m] = packed

        @pl.loop(0, levels)
        def _(k):
            z = depth(k.astype(F32))
            for g in range(groups):
                at = pl.ds(PAD + 8 * g, 8)
                rho[k, at] = density(q[0, k, at], q[1, k, at], z)

        pad_n = jnp.zeros((8, 128), I32)
        n[pl.ds(0, 8)] = pad_n
        n[pl.ds(top_row, 8)] = pad_n
        for g in range(groups):
            at = pl.ds(PAD + 8 * g, 8)
            here = n[at]
            fx = jnp.minimum(here, lanes(here, 1))
            face_x[pl.ds(8 * g, 8)] = fx
            inner = jnp.logical_and(lane > 1, lane < 127)
            keep_x[pl.ds(8 * g, 8)] = jnp.where(inner, fx, 0)
            f = jnp.minimum(here, n[pl.ds(PAD + 8 * g - 1, 8)])
            face_y[at] = f
            if g == 0:
                f = jnp.where(row > 1, f, 0)
            if g == groups - 1:
                f = jnp.where(row < 7, f, 0)
            keep_y[pl.ds(8 * g, 8)] = f
        face_y[pl.ds(0, 8)] = pad_n
        face_y[pl.ds(top_row, 8)] = pad_n

        expected = 2 + has_south.astype(I32) + has_north.astype(I32) + top.astype(I32) + top_far.astype(I32)
        pl.semaphore_wait(barrier, expected)

        def remote(src, dst, index, device, recv=None):
            return pltpu.make_async_remote_copy(
                src_ref=src, dst_ref=dst, send_sem=send_sem.at[index],
                recv_sem=recv_sem.at[index if recv is None else recv],
                device_id=device, device_id_type=MESH,
            )

        first, last = pl.ds(0, 2), pl.ds(rows - 2, 2)
        fold = pl.ds(rows - 3, 2)
        lo, hi = pl.ds(0, 2), pl.ds(6, 2)
        northward = [
            remote(t_hbm.at[:, last], h.at[0, :, lo], 0, {"lat": lat + 1}),
            remote(s_hbm.at[:, last], h.at[1, :, lo], 1, {"lat": lat + 1}),
            remote(v_hbm.at[:, last], hv.at[:, lo], 2, {"lat": lat + 1}),
            remote(n_hbm.at[last], hn.at[lo], 3, {"lat": lat + 1}),
        ]
        southward = [
            remote(t_hbm.at[:, first], h.at[0, :, hi], 4, {"lat": lat - 1}),
            remote(s_hbm.at[:, first], h.at[1, :, hi], 5, {"lat": lat - 1}),
            remote(n_hbm.at[first], hn.at[hi], 6, {"lat": lat - 1}),
        ]
        folded = [
            remote(t_hbm.at[:, fold], fa.at[0, :, hi], 7, {"lon": mirror}),
            remote(s_hbm.at[:, fold], fa.at[1, :, hi], 8, {"lon": mirror}),
            remote(n_hbm.at[fold], fan.at[hi], 9, {"lon": mirror}),
        ]
        folded_next = [
            remote(t_hbm.at[:, fold], fb.at[0, :, hi], 10, {"lon": mirror_next}),
            remote(s_hbm.at[:, fold], fb.at[1, :, hi], 11, {"lon": mirror_next}),
            remote(n_hbm.at[fold], fbn.at[hi], 12, {"lon": mirror_next}),
        ]
        own_next = [
            pltpu.make_async_copy(t_hbm.at[:, fold], fb.at[0, :, hi], load_sem.at[5]),
            pltpu.make_async_copy(s_hbm.at[:, fold], fb.at[1, :, hi], load_sem.at[6]),
            pltpu.make_async_copy(n_hbm.at[fold], fbn.at[hi], load_sem.at[7]),
        ]
        eastward = remote(px, from_w, 13, {"lon": east})
        westward = remote(px.at[pl.ds(0, 2 * packs + 1)], from_e, 14, {"lon": west})

        @pl.when(has_south)
        def _():
            for copy in southward:
                copy.start()

        @pl.when(has_north)
        def _():
            for copy in northward:
                copy.start()

        @pl.when(top)
        def _():
            for copy in folded:
                copy.start()

        @pl.when(top_far)
        def _():
            for copy in folded_next:
                copy.start()

        @pl.when(top_self)
        def _():
            for copy in own_next:
                copy.start()

        eastward.start()
        westward.start()

        outs = (t_out, s_out)
        loads[4].wait()
        fy[0, pl.ds(rows, 8)] = jnp.zeros((8, 128), F32)
        fy[1, pl.ds(rows, 8)] = jnp.zeros((8, 128), F32)

        @pl.loop(0, levels)
        def _(k):
            kp = jnp.minimum(k + 1, levels - 1)
            km = jnp.maximum(k - 1, 0)
            ends = jnp.logical_or(k == 0, k == levels - 1)
            half_scale = jnp.where(ends, 0.5, 0.25).astype(F32)

            for g in reversed(range(groups)):
                r = PAD + 8 * g
                at, dn = pl.ds(r, 8), pl.ds(r - 1, 8)
                t0 = [q[i, k, at] for i in range(2)]
                zd = [q[i, kp, at] - q[i, km, at] for i in range(2)]
                rho0 = rho[k, at]
                rz = rho[kp, at] - rho[km, at]

                wet = k < face_x[pl.ds(8 * g, 8)]
                keep = k < keep_x[pl.ds(8 * g, 8)]
                c = lanes(u[k, pl.ds(8 * g, 8)], 1)
                up, coef = courant_terms(c)
                sk = slope_term(rho0 - lanes(rho0, 1), rz + lanes(rz, 1), half_scale)
                total = []
                for i in range(2):
                    qa = lanes(t0[i], 1)
                    d = jnp.where(wet, t0[i] - qa, 0.0)
                    f = tracer_flux(keep, c, up, coef, sk, qa, t0[i], d, lanes(d, 1), lanes(d, -1), zd[i] + lanes(zd[i], 1))
                    total.append(t0[i] + (f - lanes(f, -1)))

                wet = k < face_y[at]
                wet_back = k < face_y[dn]
                wet_ahead = k < face_y[pl.ds(r + 1, 8)]
                keep = k < keep_y[pl.ds(8 * g, 8)]
                c = v[k, dn]
                up, coef = courant_terms(c)
                sk = slope_term(rho0 - rho[k, dn], rz + (rho[kp, dn] - rho[km, dn]), half_scale)
                here = k < n[at]
                for i in range(2):
                    qa = q[i, k, dn]
                    d = jnp.where(wet, t0[i] - qa, 0.0)
                    back = jnp.where(wet_back, qa - q[i, k, pl.ds(r - 2, 8)], 0.0)
                    ahead = jnp.where(wet_ahead, q[i, k, pl.ds(r + 1, 8)] - t0[i], 0.0)
                    zsum = zd[i] + (q[i, kp, dn] - q[i, km, dn])
                    f = tracer_flux(keep, c, up, coef, sk, qa, t0[i], d, back, ahead, zsum)
                    fy[i, pl.ds(8 * g, 8)] = f
                    f_north = fy[i, pl.ds(8 * g + 1, 8)]
                    outs[i][k, pl.ds(8 * g, 8)] = jnp.where(here, total[i] + (f - f_north), 0.0)

        eastward.wait_recv()
        westward.wait_recv()

        def joined(base, has_east=True):
            own = px[base]
            left = jnp.where(sl < MID, from_w[base], own)
            right = jnp.where(sl < MID, own, from_e[base]) if has_east else own
            a = jnp.where(sl < 4, lanes(left, -1), lanes(right, 4))
            b = jnp.where(sl < 4, lanes(left, -2), lanes(right, 3))
            return a, b

        na, nb = joined(2 * packs)
        face_n = jnp.minimum(na, nb)
        level_of = packs * (lane // span)
        pairs = [[joined(i * packs + m) for m in range(packs)] for i in range(2)]
        rho_pairs = []
        for m in range(packs):
            z = depth((level_of + m).astype(F32))
            rho_pairs.append([density(pairs[0][m][j], pairs[1][m][j], z) for j in range(2)])
        sums = [[a + b for a, b in one] for one in (*pairs, rho_pairs)]

        def zsum_of(one, m):
            if m < packs - 1:
                above = one[m + 1]
            else:
                above = jnp.where(lane < 128 - span, lanes(one[0], -span), one[m])
            if m > 0:
                below = one[m - 1]
            else:
                below = jnp.where(lane < span, one[0], lanes(one[packs - 1], span))
            return above - below

        used = jnp.logical_or(jnp.logical_or(sl == 1, sl == 2), jnp.logical_or(sl == 5, sl == 6))
        for m in range(packs):
            level = level_of + m
            half_scale = jnp.where(jnp.logical_or(level == 0, level == levels - 1), 0.5, 0.25)
            wet = level.astype(F32) < face_n
            keep = jnp.logical_and(wet, used)
            c = joined(2 * packs + 1 + m, False)[0]
            up, coef = courant_terms(c)
            sk = slope_term(rho_pairs[m][1] - rho_pairs[m][0], zsum_of(sums[2], m), half_scale)
            for i in range(2):
                qa, qb = pairs[i][m]
                d = jnp.where(wet, qb - qa, 0.0)
                f = tracer_flux(keep, c, up, coef, sk, qa, qb, d, lanes(d, 1), lanes(d, -1), zsum_of(sums[i], m))
                change = f - lanes(f, -1)
                ex[i, m] = jnp.where(sl < MID, lanes(change, -3), lanes(change, 2))

        ends_x = jnp.logical_or(lane < 2, lane > 125)

        @pl.loop(0, packs)
        def _(m):
            for i in range(2):
                packed = ex[i, m]
                for slot in range(16):
                    k = packs * (slot // groups) + m
                    at = pl.ds(8 * (slot % groups), 8)
                    here = jnp.logical_and(ends_x, k < n[pl.ds(PAD + 8 * (slot % groups), 8)])
                    outs[i][k, at] = outs[i][k, at] + jnp.where(here, lanes(packed, -(SLOT * slot + MID)), 0.0)

        @pl.when(jnp.logical_not(has_south))
        def _():
            hn[lo] = jnp.zeros((2, 128), I32)

            @pl.loop(0, levels)
            def _(k):
                h[0, k, lo] = jnp.zeros((2, 128), F32)
                h[1, k, lo] = jnp.zeros((2, 128), F32)
                hv[k, lo] = jnp.zeros((2, 128), F32)

        @pl.when(has_south)
        def _():
            for copy in northward:
                copy.wait_recv()

        @pl.when(has_north)
        def _():
            for copy in southward:
                copy.wait_recv()

        @pl.when(top)
        def _():
            for copy in folded:
                copy.wait_recv()

        @pl.when(top_far)
        def _():
            for copy in folded_next:
                copy.wait_recv()

        @pl.when(top_self)
        def _():
            for copy in own_next:
                copy.wait()

        @pl.when(top)
        def _():
            order = lax.rem(128 - lane, 128)

            def mirrored(a, b):
                x = jnp.where(lane == 0, b, a)
                x = jnp.where(row == 6, rows_by(x, -1), rows_by(x, 1))
                return jnp.take_along_axis(x, order, axis=1)

            hn[hi] = mirrored(fan[...].astype(F32), fbn[...].astype(F32))[6:8].astype(I32)

            @pl.loop(0, levels)
            def _(k):
                for i in range(2):
                    h[i, k, hi] = mirrored(fa[i, k], fb[i, k])[6:8]

        def edge_pair(halo, load):
            a = jnp.where(
                row < 2, halo, jnp.where(row < 4, load(PAD - 2), jnp.where(row < 7, load(top_row - 7), rows_by(halo, 1)))
            )
            b = jnp.where(
                row < 1, rows_by(halo, -1), jnp.where(row < 4, load(PAD - 1), jnp.where(row < 6, load(top_row - 6), halo))
            )
            return a, b

        na, nb = edge_pair(hn[...], lambda at: n[pl.ds(at, 8)])
        face_n = jnp.minimum(na, nb)
        used_y = jnp.logical_or(jnp.logical_or(row == 1, row == 2), jnp.logical_or(row == 5, row == 6))

        @pl.loop(0, levels)
        def _(k):
            z = depth(k.astype(F32))
            pair = [edge_pair(h[i, k], lambda at, i=i: q[i, k, pl.ds(at, 8)]) for i in range(2)]
            ra, rb = [density(pair[0][j], pair[1][j], z) for j in range(2)]
            for i in range(2):
                ey[2 * i, k] = pair[i][0]
                ey[2 * i + 1, k] = pair[i][1]
                ey[4 + i, k] = pair[i][0] + pair[i][1]
            ey[6, k] = ra + rb
            ey[7, k] = rb - ra

        @pl.loop(0, levels)
        def _(k):
            kp = jnp.minimum(k + 1, levels - 1)
            km = jnp.maximum(k - 1, 0)
            ends = jnp.logical_or(k == 0, k == levels - 1)
            half_scale = jnp.where(ends, 0.5, 0.25).astype(F32)
            wet = k < face_n
            keep = jnp.logical_and(wet, used_y)
            c = jnp.where(row < 2, hv[k], jnp.where(row < 4, v[k, pl.ds(PAD - 2, 8)], v[k, pl.ds(top_row - 7, 8)]))
            up, coef = courant_terms(c)
            sk = slope_term(ey[7, k], ey[6, kp] - ey[6, km], half_scale)
            south, north = pl.ds(0, 8), pl.ds(rows - 8, 8)
            here_s = jnp.logical_and(row < 2, k < n[pl.ds(PAD, 8)])
            here_n = jnp.logical_and(row > 5, k < n[pl.ds(top_row - 8, 8)])
            for i in range(2):
                qa, qb = ey[2 * i, k], ey[2 * i + 1, k]
                d = jnp.where(wet, qb - qa, 0.0)
                zsum = ey[4 + i, kp] - ey[4 + i, km]
                f = tracer_flux(keep, c, up, coef, sk, qa, qb, d, rows_by(d, 1), rows_by(d, -1), zsum)
                change = f - rows_by(f, -1)
                outs[i][k, south] = outs[i][k, south] + jnp.where(here_s, rows_by(change, -1), 0.0)
                outs[i][k, north] = outs[i][k, north] + jnp.where(here_n, rows_by(change, 2), 0.0)

        eastward.wait_send()
        westward.wait_send()

        @pl.when(has_south)
        def _():
            for copy in southward:
                copy.wait_send()

        @pl.when(has_north)
        def _():
            for copy in northward:
                copy.wait_send()

        @pl.when(top)
        def _():
            for copy in folded:
                copy.wait_send()

        @pl.when(top_far)
        def _():
            for copy in folded_next:
                copy.wait_send()

    return kernel


def solution(mesh):
    nlon, nlat = mesh.shape["lon"], mesh.shape["lat"]

    def body(t, s, u, v, n):
        levels, rows, cols = t.shape
        packs = levels // (16 // (rows // 8))
        tall = rows + 2 * PAD
        tile = jax.ShapeDtypeStruct((levels, rows, cols), F32)
        return pl.pallas_call(
            make_kernel(nlon, nlat, levels, rows),
            out_shape=(tile, tile),
            in_specs=[pl.BlockSpec(memory_space=pl.ANY)] * 5,
            out_specs=(pl.BlockSpec(memory_space=pltpu.VMEM),) * 2,
            scratch_shapes=[
                pltpu.VMEM((2, levels, tall, cols), F32),
                pltpu.VMEM((levels, tall, cols), F32),
                pltpu.VMEM((levels, rows, cols), F32),
                pltpu.VMEM((levels, tall, cols), F32),
                pltpu.VMEM((tall, cols), I32),
                pltpu.VMEM((rows, cols), I32),
                pltpu.VMEM((rows, cols), I32),
                pltpu.VMEM((tall, cols), I32),
                pltpu.VMEM((rows, cols), I32),
                pltpu.VMEM((2, rows + 8, cols), F32),
                pltpu.VMEM((3 * packs + 1, 8, cols), F32),
                pltpu.VMEM((3 * packs + 1, 8, cols), F32),
                pltpu.VMEM((2 * packs + 1, 8, cols), F32),
                pltpu.VMEM((2, levels, 8, cols), F32),
                pltpu.VMEM((levels, 8, cols), F32),
                pltpu.VMEM((8, cols), I32),
                pltpu.VMEM((2, levels, 8, cols), F32),
                pltpu.VMEM((2, levels, 8, cols), F32),
                pltpu.VMEM((8, cols), I32),
                pltpu.VMEM((8, cols), I32),
                pltpu.VMEM((2, packs, 8, cols), F32),
                pltpu.VMEM((8, levels, 8, cols), F32),
                pltpu.SemaphoreType.DMA((8,)),
                pltpu.SemaphoreType.DMA((15,)),
                pltpu.SemaphoreType.DMA((15,)),
            ],
            compiler_params=pltpu.CompilerParams(collective_id=0, has_side_effects=True),
            name="tracer_step",
        )(t, s, u, v, n)

    spec = P(None, "lat", "lon")
    return jax.shard_map(
        body, mesh=mesh, in_specs=(spec,) * 4 + (P("lat", "lon"),), out_specs=(spec, spec), check_vma=False
    )
```

time: 126 us -> 20 us (0.16); the launches traced: 123 us -> 19.8 us
  waiting for transfers between devices: 49 us -> 0 us
  local copies, waits for them, and re-layouts: 31.8 us -> 2.42 us
  Pallas kernels: 0 us -> 16.7 us
  starting transfers between devices: 15.1 us -> 0 us
  between operations: 14.4 us -> 0.65 us
  other arithmetic: 13.1 us -> 0 us
    all_gather x1 -> x0, waiting for transfers between devices: 38.6 us -> none  [body(): lax.all_gather(scalar_quantities[:3, :, latitude_band_sum - 3:, :], 'lon'...]
    rev x2 -> x0, local copies, waits for them, and re-layouts: 22.7 us -> none  [body(): flipped = jnp.flip(whole_rows, -1)]
    pallas_call x0 -> x1, Pallas kernels: none -> 16.7 us  [body(): pl.pallas_call(make_kernel(nlon, nlat, levels, rows), out_shape=(tile, ti...]
    ppermute x6 -> x0, starting transfers between devices: 15 us -> none  [the longest x2 12.1 us: extended(): after = lax.ppermute(first, axis, down)]
    ppermute x6 -> x0, waiting for transfers between devices: 10.5 us -> none  [the longest x2 5.88 us: extended(): before = lax.ppermute(last, axis, up)]
    max x2 -> x0, other arithmetic: 2.84 us -> none  [face_flux(): positive = jnp.maximum(face_speed, 0.0)]
    mul x10 -> x0, other arithmetic: 2.7 us -> none  [the longest x2 0.96 us: face_flux(): slope_face * vert_face]
    add x2 -> x0, other arithmetic: 2.4 us -> none  [face_flux(): flux_total = advective + isoneutral]
  transfers between devices with their start and end apart: 7 -> 0, of which waited for: 4 -> 0; matrix products, arithmetic and copies ran while one was open for 6% -> 0% of each run, Pallas kernels for 0% -> 0%
where the time goes in v1:
time: 20 us; the launch traced here: 19.8 us
  Pallas kernels  16.7 us (84%)
  local copies, waits for them, and re-layouts  2.42 us (12%)
  between operations  0.65 us (3%)
    pallas_call x1, Pallas kernels, body(): pl.pallas_call(make_kernel(nlon, nlat, levels, rows), out_shape=(tile, ti...  16.7 us
    unnamed x4, local copies, waits for them, and re-layouts  2.42 us

profile of v1, /device:TPU:28, one launch (start us, length us, event | category | flops | bytes accessed | tf_op | source)
XLA Modules:
  0.0 19.8 jit_solution(9707724277213774719)
XLA Ops:
  0.6 16.7 %tracer_step.1 = (f32[16,32,128]{2,1,0:T(8,128)}, f32[16,32,128]{2,1,0:T(8,128)}) custom-call(f32[16,32,128]{2,1,0:T(8,128)} %t_hbm.1, f32[16,32,128]{2,1,0:T(8,128)} %s_hbm.1, f32[16,32,128]{2,1,0:T(8,128)} %u_hbm.1, f32[16,32,128]{2,1,0:T(8,128)} %v_hbm.1, s32[32,128]{1,0:T(8,128)} %n_hbm.1), custom_call_target="tpu_custom_call" | custom-call | tf_op jit(solution)/shard_map/tracer_step/pallas_call | solution.py:496
  17.4 0.0 copy-start
  17.4 1.7 %copy.9 = f32[16,32,128]{2,1,0:T(8,128)} copy(f32[16,32,128]{2,1,0:T(8,128)} %get-tuple-element.4) | data formatting | bytes 524288
  19.1 0.0 copy-done
  19.1 0.7 %copy.10 = f32[16,32,128]{2,1,0:T(8,128)} copy(f32[16,32,128]{2,1,0:T(8,128)S(1)} %copy-done) | data formatting | bytes 524288
Async XLA Ops:
  17.4 1.7 %copy-start = (f32[16,32,128]{2,1,0:T(8,128)S(1)}, f32[16,32,128]{2,1,0:T(8,128)}, u32[]{:S(2)}) copy-start(f32[16,32,128]{2,1,0:T(8,128)} %get-tuple-element.5) | copy-start | bytes 786436

commit v2 on v1

--- a/solution.py
+++ b/solution.py
@@ -70,9 +70,10 @@
         return TOTAL_DEPTH * (k + 0.5) / levels
 
     def kernel(
-        t_hbm, s_hbm, u_hbm, v_hbm, n_hbm, t_out, s_out,
-        q, rho, u, v, n, face_x, keep_x, face_y, keep_y, fy,
-        px, from_w, from_e, h, hv, hn, fa, fb, fan, fbn, ex, ey,
+        t_hbm, s_hbm, u_hbm, v_hbm, n_hbm,
+        t_out, s_out, q, v, n, h, hv, hn,
+        rho, u, face_x, keep_x, face_y, keep_y, fy,
+        px, to_e, to_w, from_w, from_e, fa, fb, fan, ex,
         load_sem, send_sem, recv_sem,
     ):
         lon = lax.axis_index("lon")
@@ -128,20 +129,69 @@
         slot_of = lane // SLOT
         sl = lane % SLOT
 
-        loads[0].wait()
+        expected = 2 + has_south.astype(I32) + has_north.astype(I32) + top.astype(I32) + top_far.astype(I32)
+        pl.semaphore_wait(barrier, expected)
+
+        def remote(src, dst, index, device):
+            return pltpu.make_async_remote_copy(
+                src_ref=src, dst_ref=dst, send_sem=send_sem.at[index], recv_sem=recv_sem.at[index],
+                device_id=device, device_id_type=MESH,
+            )
+
+        first, last = pl.ds(0, 2), pl.ds(rows - 2, 2)
+        fold = pl.ds(rows - 3, 2)
+        fold_in_group = pl.ds(5, 2)
+        lo, hi = pl.ds(0, 2), pl.ds(6, 2)
+        northward = [
+            remote(t_hbm.at[:, last], h.at[0, :, lo], 0, {"lat": lat + 1}),
+            remote(s_hbm.at[:, last], h.at[1, :, lo], 1, {"lat": lat + 1}),
+            remote(v_hbm.at[:, pl.ds(rows - 1, 1)], hv.at[:, pl.ds(1, 1)], 2, {"lat": lat + 1}),
+            remote(n_hbm.at[last], hn.at[lo], 3, {"lat": lat + 1}),
+        ]
+        southward = [
+            remote(t_hbm.at[:, first], h.at[0, :, hi], 4, {"lat": lat - 1}),
+            remote(s_hbm.at[:, first], h.at[1, :, hi], 5, {"lat": lat - 1}),
+            remote(n_hbm.at[first], hn.at[hi], 6, {"lat": lat - 1}),
+        ]
+        folded = [
+            remote(t_hbm.at[:, fold], fa.at[0, :, hi], 7, {"lon": mirror}),
+            remote(s_hbm.at[:, fold], fa.at[1, :, hi], 8, {"lon": mirror}),
+            remote(n_hbm.at[fold], fan.at[hi], 9, {"lon": mirror}),
+        ]
+        folded_next = remote(to_w.at[:, fold_in_group], fb.at[:, hi], 10, {"lon": mirror_next})
+        own_next = pltpu.make_async_copy(to_w.at[:, fold_in_group], fb.at[:, hi], load_sem.at[5])
+        eastward = remote(to_e, from_w, 11, {"lon": east})
+        westward = remote(to_w, from_e, 12, {"lon": west})
+
+        @pl.when(top)
+        def _():
+            for copy in folded:
+                copy.start()
+
+        @pl.when(has_south)
+        def _():
+            for copy in southward:
+                copy.start()
+
+        @pl.when(has_north)
+        def _():
+            for copy in northward:
+                copy.start()
+
+        for load in loads[:4]:
+            load.wait()
         packed_n = jnp.zeros((8, 128), F32)
         for slot in range(16):
             part = n[pl.ds(PAD + 8 * (slot % groups), 8)].astype(F32)
             packed_n = jnp.where(slot_of == slot, lanes(part, SLOT * slot + MID), packed_n)
         px[2 * packs] = packed_n
-        loads[1].wait()
-        loads[2].wait()
-        loads[3].wait()
+        n_up, n_down = lanes(packed_n, 5), lanes(packed_n, -2)
 
         @pl.loop(0, packs)
         def _(m):
+            packed = []
             for field in range(3):
-                packed = jnp.zeros((8, 128), F32)
+                one = jnp.zeros((8, 128), F32)
                 for slot in range(16):
                     k = packs * (slot // groups) + m
                     g = slot % groups
@@ -149,8 +199,24 @@
                         part = q[field, k, pl.ds(PAD + 8 * g, 8)]
                     else:
                         part = u[k, pl.ds(8 * g, 8)]
-                    packed = jnp.where(slot_of == slot, lanes(part, SLOT * slot + MID), packed)
-                px[(0, packs, 2 * packs + 1)[field] + m] = packed
+                    one = jnp.where(slot_of == slot, lanes(part, SLOT * slot + MID), one)
+                px[(0, packs, 2 * packs + 1)[field] + m] = one
+                packed.append(one)
+            t2, s2, u2 = packed
+            s_up = lanes(s2, 2)
+            to_e[m] = jnp.where(sl < 3, t2, jnp.where(sl < 5, s_up, jnp.where(sl < 6, lanes(u2, 3), n_up)))
+            to_w[m] = jnp.where(sl < 3, n_down, jnp.where(sl < 5, t2, s_up))
+
+        @pl.when(top_far)
+        def _():
+            folded_next.start()
+
+        @pl.when(top_self)
+        def _():
+            own_next.start()
+
+        eastward.start()
+        westward.start()
 
         @pl.loop(0, levels)
         def _(k):
@@ -179,76 +245,6 @@
         face_y[pl.ds(0, 8)] = pad_n
         face_y[pl.ds(top_row, 8)] = pad_n
 
-        expected = 2 + has_south.astype(I32) + has_north.astype(I32) + top.astype(I32) + top_far.astype(I32)
-        pl.semaphore_wait(barrier, expected)
-
-        def remote(src, dst, index, device, recv=None):
-            return pltpu.make_async_remote_copy(
-                src_ref=src, dst_ref=dst, send_sem=send_sem.at[index],
-                recv_sem=recv_sem.at[index if recv is None else recv],
-                device_id=device, device_id_type=MESH,
-            )
-
-        first, last = pl.ds(0, 2), pl.ds(rows - 2, 2)
-        fold = pl.ds(rows - 3, 2)
-        lo, hi = pl.ds(0, 2), pl.ds(6, 2)
-        northward = [
-            remote(t_hbm.at[:, last], h.at[0, :, lo], 0, {"lat": lat + 1}),
-            remote(s_hbm.at[:, last], h.at[1, :, lo], 1, {"lat": lat + 1}),
-            remote(v_hbm.at[:, last], hv.at[:, lo], 2, {"lat": lat + 1}),
-            remote(n_hbm.at[last], hn.at[lo], 3, {"lat": lat + 1}),
-        ]
-        southward = [
-            remote(t_hbm.at[:, first], h.at[0, :, hi], 4, {"lat": lat - 1}),
-            remote(s_hbm.at[:, first], h.at[1, :, hi], 5, {"lat": lat - 1}),
-            remote(n_hbm.at[first], hn.at[hi], 6, {"lat": lat - 1}),
-        ]
-        folded = [
-            remote(t_hbm.at[:, fold], fa.at[0, :, hi], 7, {"lon": mirror}),
-            remote(s_hbm.at[:, fold], fa.at[1, :, hi], 8, {"lon": mirror}),
-            remote(n_hbm.at[fold], fan.at[hi], 9, {"lon": mirror}),
-        ]
-        folded_next = [
-            remote(t_hbm.at[:, fold], fb.at[0, :, hi], 10, {"lon": mirror_next}),
-            remote(s_hbm.at[:, fold], fb.at[1, :, hi], 11, {"lon": mirror_next}),
-            remote(n_hbm.at[fold], fbn.at[hi], 12, {"lon": mirror_next}),
-        ]
-        own_next = [
-            pltpu.make_async_copy(t_hbm.at[:, fold], fb.at[0, :, hi], load_sem.at[5]),
-            pltpu.make_async_copy(s_hbm.at[:, fold], fb.at[1, :, hi], load_sem.at[6]),
-            pltpu.make_async_copy(n_hbm.at[fold], fbn.at[hi], load_sem.at[7]),
-        ]
-        eastward = remote(px, from_w, 13, {"lon": east})
-        westward = remote(px.at[pl.ds(0, 2 * packs + 1)], from_e, 14, {"lon": west})
-
-        @pl.when(has_south)
-        def _():
-            for copy in southward:
-                copy.start()
-
-        @pl.when(has_north)
-        def _():
-            for copy in northward:
-                copy.start()
-
-        @pl.when(top)
-        def _():
-            for copy in folded:
-                copy.start()
-
-        @pl.when(top_far)
-        def _():
-            for copy in folded_next:
-                copy.start()
-
-        @pl.when(top_self)
-        def _():
-            for copy in own_next:
-                copy.start()
-
-        eastward.start()
-        westward.start()
-
         outs = (t_out, s_out)
         loads[4].wait()
         fy[0, pl.ds(rows, 8)] = jnp.zeros((8, 128), F32)
@@ -303,18 +299,20 @@
         eastward.wait_recv()
         westward.wait_recv()
 
-        def joined(base, has_east=True):
-            own = px[base]
-            left = jnp.where(sl < MID, from_w[base], own)
-            right = jnp.where(sl < MID, own, from_e[base]) if has_east else own
+        def joined(own, before, after):
+            left = jnp.where(sl < MID, before, own)
+            right = own if after is None else jnp.where(sl < MID, own, after)
             a = jnp.where(sl < 4, lanes(left, -1), lanes(right, 4))
             b = jnp.where(sl < 4, lanes(left, -2), lanes(right, 3))
             return a, b
 
-        na, nb = joined(2 * packs)
+        na, nb = joined(px[2 * packs], lanes(from_w[0], -5), lanes(from_e[0], 2))
         face_n = jnp.minimum(na, nb)
         level_of = packs * (lane // span)
-        pairs = [[joined(i * packs + m) for m in range(packs)] for i in range(2)]
+        pairs = [
+            [joined(px[m], from_w[m], from_e[m]) for m in range(packs)],
+            [joined(px[packs + m], lanes(from_w[m], -2), lanes(from_e[m], -2)) for m in range(packs)],
+        ]
         rho_pairs = []
         for m in range(packs):
             z = depth((level_of + m).astype(F32))
@@ -338,7 +336,7 @@
             half_scale = jnp.where(jnp.logical_or(level == 0, level == levels - 1), 0.5, 0.25)
             wet = level.astype(F32) < face_n
             keep = jnp.logical_and(wet, used)
-            c = joined(2 * packs + 1 + m, False)[0]
+            c = joined(px[2 * packs + 1 + m], lanes(from_w[m], -3), None)[0]
             up, coef = courant_terms(c)
             sk = slope_term(rho_pairs[m][1] - rho_pairs[m][0], zsum_of(sums[2], m), half_scale)
             for i in range(2):
@@ -387,29 +385,72 @@
 
         @pl.when(top_far)
         def _():
-            for copy in folded_next:
-                copy.wait_recv()
+            folded_next.wait_recv()
 
         @pl.when(top_self)
         def _():
-            for copy in own_next:
-                copy.wait()
+            own_next.wait()
 
         @pl.when(top)
         def _():
             order = lax.rem(128 - lane, 128)
 
-            def mirrored(a, b):
-                x = jnp.where(lane == 0, b, a)
+            def mirrored(x):
                 x = jnp.where(row == 6, rows_by(x, -1), rows_by(x, 1))
                 return jnp.take_along_axis(x, order, axis=1)
 
-            hn[hi] = mirrored(fan[...].astype(F32), fbn[...].astype(F32))[6:8].astype(I32)
-
-            @pl.loop(0, levels)
-            def _(k):
-                for i in range(2):
-                    h[i, k, hi] = mirrored(fa[i, k], fb[i, k])[6:8]
+            spot = SLOT * (groups - 1) + MID
+            x = jnp.where(lane == 0, lanes(fb[0], -(spot - 2)), fan[...].astype(F32))
+            hn[hi] = mirrored(x)[6:8].astype(I32)
+
+            @pl.loop(0, packs)
+            def _(m):
+                for part in range(16 // groups):
+                    k = packs * part + m
+                    for i in range(2):
+                        x = jnp.where(lane == 0, lanes(fb[m], -(span * part + spot + 2 * i)), fa[i, k])
+                        h[i, k, hi] = mirrored(x)[6:8]
+
+        eastward.wait_send()
+        westward.wait_send()
+
+        @pl.when(has_south)
+        def _():
+            for copy in southward:
+                copy.wait_send()
+
+        @pl.when(has_north)
+        def _():
+            for copy in northward:
+                copy.wait_send()
+
+        @pl.when(top)
+        def _():
+            for copy in folded:
+                copy.wait_send()
+
+        @pl.when(top_far)
+        def _():
+            folded_next.wait_send()
+
+    return kernel
+
+
+def make_edge_kernel(levels, rows):
+    top_row = PAD + rows
+    unroll = 4
+
+    def kernel(t_part, s_part, q, v, n, h, hv, hn, t_out, s_out, ey, done, sem):
+        parts = (t_part, s_part)
+        outs = (t_out, s_out)
+        row = lax.broadcasted_iota(I32, (8, 128), 0)
+        inner = pl.ds(8, rows - 16)
+        south, north = pl.ds(0, 8), pl.ds(rows - 8, 8)
+        stores = [
+            pltpu.make_async_copy(parts[i].at[:, inner], outs[i].at[:, inner], sem.at[i]) for i in range(2)
+        ]
+        for store in stores:
+            store.start()
 
         def edge_pair(halo, load):
             a = jnp.where(
@@ -422,65 +463,54 @@
 
         na, nb = edge_pair(hn[...], lambda at: n[pl.ds(at, 8)])
         face_n = jnp.minimum(na, nb)
-        used_y = jnp.logical_or(jnp.logical_or(row == 1, row == 2), jnp.logical_or(row == 5, row == 6))
-
-        @pl.loop(0, levels)
-        def _(k):
-            z = depth(k.astype(F32))
-            pair = [edge_pair(h[i, k], lambda at, i=i: q[i, k, pl.ds(at, 8)]) for i in range(2)]
-            ra, rb = [density(pair[0][j], pair[1][j], z) for j in range(2)]
-            for i in range(2):
-                ey[2 * i, k] = pair[i][0]
-                ey[2 * i + 1, k] = pair[i][1]
-                ey[4 + i, k] = pair[i][0] + pair[i][1]
-            ey[6, k] = ra + rb
-            ey[7, k] = rb - ra
-
-        @pl.loop(0, levels)
-        def _(k):
-            kp = jnp.minimum(k + 1, levels - 1)
-            km = jnp.maximum(k - 1, 0)
-            ends = jnp.logical_or(k == 0, k == levels - 1)
-            half_scale = jnp.where(ends, 0.5, 0.25).astype(F32)
-            wet = k < face_n
-            keep = jnp.logical_and(wet, used_y)
-            c = jnp.where(row < 2, hv[k], jnp.where(row < 4, v[k, pl.ds(PAD - 2, 8)], v[k, pl.ds(top_row - 7, 8)]))
-            up, coef = courant_terms(c)
-            sk = slope_term(ey[7, k], ey[6, kp] - ey[6, km], half_scale)
-            south, north = pl.ds(0, 8), pl.ds(rows - 8, 8)
-            here_s = jnp.logical_and(row < 2, k < n[pl.ds(PAD, 8)])
-            here_n = jnp.logical_and(row > 5, k < n[pl.ds(top_row - 8, 8)])
-            for i in range(2):
-                qa, qb = ey[2 * i, k], ey[2 * i + 1, k]
-                d = jnp.where(wet, qb - qa, 0.0)
-                zsum = ey[4 + i, kp] - ey[4 + i, km]
-                f = tracer_flux(keep, c, up, coef, sk, qa, qb, d, rows_by(d, 1), rows_by(d, -1), zsum)
-                change = f - rows_by(f, -1)
-                outs[i][k, south] = outs[i][k, south] + jnp.where(here_s, rows_by(change, -1), 0.0)
-                outs[i][k, north] = outs[i][k, north] + jnp.where(here_n, rows_by(change, 2), 0.0)
-
-        eastward.wait_send()
-        westward.wait_send()
-
-        @pl.when(has_south)
-        def _():
-            for copy in southward:
-                copy.wait_send()
-
-        @pl.when(has_north)
-        def _():
-            for copy in northward:
-                copy.wait_send()
-
-        @pl.when(top)
-        def _():
-            for copy in folded:
-                copy.wait_send()
-
-        @pl.when(top_far)
-        def _():
-            for copy in folded_next:
-                copy.wait_send()
+        used = jnp.logical_or(jnp.logical_or(row == 1, row == 2), jnp.logical_or(row == 5, row == 6))
+
+        @pl.loop(0, levels // unroll)
+        def _(block):
+            for j in range(unroll):
+                k = block * unroll + j
+                z = TOTAL_DEPTH * (k.astype(F32) + 0.5) / levels
+                pair = [edge_pair(h[i, k], lambda at, i=i: q[i, k, pl.ds(at, 8)]) for i in range(2)]
+                ra, rb = [density(pair[0][j], pair[1][j], z) for j in range(2)]
+                for i in range(2):
+                    ey[2 * i, k] = pair[i][0]
+                    ey[2 * i + 1, k] = pair[i][1]
+                    ey[4 + i, k] = pair[i][0] + pair[i][1]
+                ey[6, k] = ra + rb
+                ey[7, k] = rb - ra
+
+        n_south = jnp.where(row < 2, n[pl.ds(PAD, 8)], 0)
+        n_north = jnp.where(row > 5, n[pl.ds(top_row - 8, 8)], 0)
+
+        @pl.loop(0, levels // unroll)
+        def _(block):
+            for j in range(unroll):
+                k = block * unroll + j
+                kp = jnp.minimum(k + 1, levels - 1)
+                km = jnp.maximum(k - 1, 0)
+                ends = jnp.logical_or(k == 0, k == levels - 1)
+                half_scale = jnp.where(ends, 0.5, 0.25).astype(F32)
+                wet = k < face_n
+                keep = jnp.logical_and(wet, used)
+                c = jnp.where(row < 2, hv[k], jnp.where(row < 4, v[k, pl.ds(PAD - 2, 8)], v[k, pl.ds(top_row - 7, 8)]))
+                up, coef = courant_terms(c)
+                sk = slope_term(ey[7, k], ey[6, kp] - ey[6, km], half_scale)
+                for i in range(2):
+                    qa, qb = ey[2 * i, k], ey[2 * i + 1, k]
+                    d = jnp.where(wet, qb - qa, 0.0)
+                    zsum = ey[4 + i, kp] - ey[4 + i, km]
+                    f = tracer_flux(keep, c, up, coef, sk, qa, qb, d, rows_by(d, 1), rows_by(d, -1), zsum)
+                    change = f - rows_by(f, -1)
+                    done[2 * i, k] = parts[i][k, south] + jnp.where(k < n_south, rows_by(change, -1), 0.0)
+                    done[2 * i + 1, k] = parts[i][k, north] + jnp.where(k < n_north, rows_by(change, 2), 0.0)
+
+        for i in range(2):
+            stores.append(pltpu.make_async_copy(done.at[2 * i], outs[i].at[:, south], sem.at[2 + 2 * i]))
+            stores.append(pltpu.make_async_copy(done.at[2 * i + 1], outs[i].at[:, north], sem.at[3 + 2 * i]))
+        for store in stores[2:]:
+            store.start()
+        for store in stores:
+            store.wait()
 
     return kernel
 
@@ -492,42 +522,57 @@
         levels, rows, cols = t.shape
         packs = levels // (16 // (rows // 8))
         tall = rows + 2 * PAD
-        tile = jax.ShapeDtypeStruct((levels, rows, cols), F32)
-        return pl.pallas_call(
+        plain = jax.ShapeDtypeStruct((levels, rows, cols), F32)
+        parts = pl.pallas_call(
             make_kernel(nlon, nlat, levels, rows),
-            out_shape=(tile, tile),
-            in_specs=[pl.BlockSpec(memory_space=pl.ANY)] * 5,
-            out_specs=(pl.BlockSpec(memory_space=pltpu.VMEM),) * 2,
-            scratch_shapes=[
+            out_shape=(
+                pltpu.VMEM((levels, rows, cols), F32),
+                pltpu.VMEM((levels, rows, cols), F32),
                 pltpu.VMEM((2, levels, tall, cols), F32),
                 pltpu.VMEM((levels, tall, cols), F32),
+                pltpu.VMEM((tall, cols), I32),
+                pltpu.VMEM((2, levels, 8, cols), F32),
+                pltpu.VMEM((levels, 8, cols), F32),
+                pltpu.VMEM((8, cols), I32),
+            ),
+            in_specs=[pl.BlockSpec(memory_space=pl.ANY)] * 5,
+            out_specs=(pl.BlockSpec(memory_space=pltpu.VMEM),) * 8,
+            scratch_shapes=[
+                pltpu.VMEM((levels, tall, cols), F32),
                 pltpu.VMEM((levels, rows, cols), F32),
-                pltpu.VMEM((levels, tall, cols), F32),
-                pltpu.VMEM((tall, cols), I32),
                 pltpu.VMEM((rows, cols), I32),
                 pltpu.VMEM((rows, cols), I32),
                 pltpu.VMEM((tall, cols), I32),
                 pltpu.VMEM((rows, cols), I32),
                 pltpu.VMEM((2, rows + 8, cols), F32),
                 pltpu.VMEM((3 * packs + 1, 8, cols), F32),
-                pltpu.VMEM((3 * packs + 1, 8, cols), F32),
-                pltpu.VMEM((2 * packs + 1, 8, cols), F32),
+                pltpu.VMEM((packs, 8, cols), F32),
+                pltpu.VMEM((packs, 8, cols), F32),
+                pltpu.VMEM((packs, 8, cols), F32),
+                pltpu.VMEM((packs, 8, cols), F32),
                 pltpu.VMEM((2, levels, 8, cols), F32),
-                pltpu.VMEM((levels, 8, cols), F32),
-                pltpu.VMEM((8, cols), I32),
-                pltpu.VMEM((2, levels, 8, cols), F32),
-                pltpu.VMEM((2, levels, 8, cols), F32),
-                pltpu.VMEM((8, cols), I32),
+                pltpu.VMEM((packs, 8, cols), F32),
                 pltpu.VMEM((8, cols), I32),
                 pltpu.VMEM((2, packs, 8, cols), F32),
-                pltpu.VMEM((8, levels, 8, cols), F32),
-                pltpu.SemaphoreType.DMA((8,)),
-                pltpu.SemaphoreType.DMA((15,)),
-                pltpu.SemaphoreType.DMA((15,)),
+                pltpu.SemaphoreType.DMA((6,)),
+                pltpu.SemaphoreType.DMA((13,)),
+                pltpu.SemaphoreType.DMA((13,)),
             ],
             compiler_params=pltpu.CompilerParams(collective_id=0, has_side_effects=True),
             name="tracer_step",
         )(t, s, u, v, n)
+        return pl.pallas_call(
+            make_edge_kernel(levels, rows),
+            out_shape=(plain, plain),
+            in_specs=[pl.BlockSpec(memory_space=pltpu.VMEM)] * 8,
+            out_specs=(pl.BlockSpec(memory_space=pl.ANY),) * 2,
+            scratch_shapes=[
+                pltpu.VMEM((8, levels, 8, cols), F32),
+                pltpu.VMEM((4, levels, 8, cols), F32),
+                pltpu.SemaphoreType.DMA((6,)),
+            ],
+            name="edge_rows",
+        )(*[pltpu.with_memory_space_constraint(part, pltpu.VMEM) for part in parts])
 
     spec = P(None, "lat", "lon")
     return jax.shard_map(

time: 20 us -> 15.7 us (0.78)
  the two profiles are of different devices: /device:TPU:28 before, /device:TPU:29 now
where the time goes in v2:
time: 15.7 us; the launch traced here: 15.5 us
  Pallas kernels  14.9 us (95%)
  between operations  0.64 us (4%)
    pallas_call x1, Pallas kernels, body(): pl.pallas_call(make_kernel(nlon, nlat, levels, rows), out_shape=(pltpu.VM...  13.8 us
    pallas_call x1, Pallas kernels, body(): pl.pallas_call(make_edge_kernel(levels, rows), out_shape=(plain, plain),...  1.08 us

profile of v2, /device:TPU:29, one launch (start us, length us, event | category | flops | bytes accessed | tf_op | source)
XLA Modules:
  0.0 15.5 jit_solution(17991340636013330300)
XLA Ops:
  0.6 13.8 %tracer_step.1 = (f32[16,32,128]{2,1,0:T(8,128)S(1)}, f32[16,32,128]{2,1,0:T(8,128)S(1)}, f32[2,16,48,128]{3,2,1,0:T(8,128)S(1)}, f32[16,48,128]{2,1,0:T(8,128)S...) custom-call(f32[16,32,128]{2,1,0:T(8,128)} %t_hbm.1, ...), custom_call_target="tpu_custom_call" | custom-call | tf_op jit(solution)/shard_map/tracer_step/pallas_call | solution.py:526
  14.4 1.1 %edge_rows.1 = (f32[16,32,128]{2,1,0:T(8,128)}, f32[16,32,128]{2,1,0:T(8,128)}) custom-call(f32[16,32,128]{2,1,0:T(8,128)S(1)} %get-tuple-element.10.t_part, f32[16,32,128]{2,1,0:T(8,128)S(1)} %get-tuple-element.11.s_part, f32[2,16,48,128]{3,2,1,0:T(8,128)S(1)} %get-tuple-element.12.q, f32[16,48,128]{2,1,0:T(8,128)S(1)} %get-tuple-element.13.v, ...), custom_call_target="tpu_custom_call" | custom-call | tf_op jit(solution)/shard_map/edge_rows/pallas_call | solution.py:564

commit v3 on v2

--- a/solution.py
+++ b/solution.py
@@ -74,7 +74,7 @@
         t_out, s_out, q, v, n, h, hv, hn,
         rho, u, face_x, keep_x, face_y, keep_y, fy,
         px, to_e, to_w, from_w, from_e, fa, fb, fan, ex,
-        load_sem, send_sem, recv_sem,
+        load_sem, send_sem, recv_sem, late_ready,
     ):
         lon = lax.axis_index("lon")
         lat = lax.axis_index("lat")
@@ -88,30 +88,39 @@
         mirror_far = mirror_next != lon
         top_far = jnp.logical_and(top, mirror_far)
         top_self = jnp.logical_and(top, jnp.logical_not(mirror_far))
+        half, quarter = nlon // 2, nlon // 4
+        place = lax.rem(lon, half)
+        early = place < quarter
+        late_west = place == 0
+        late_east = place == quarter - 1
+        early_west = place == quarter
+        early_east = place == half - 1
+        mirror_late = jnp.logical_and(top, early)
+        mirror_early = jnp.logical_and(top, jnp.logical_not(early))
+        next_late = jnp.logical_and(top_far, early)
+        next_early = jnp.logical_and(top_far, place > quarter)
+        next_same = jnp.logical_and(top_far, place == quarter)
 
         barrier = pltpu.get_barrier_semaphore()
 
         def greet(device):
             pl.semaphore_signal(barrier, inc=1, device_id=device, device_id_type=MESH)
 
-        @pl.when(has_south)
-        def _():
-            greet({"lat": lat - 1})
-
-        @pl.when(has_north)
-        def _():
-            greet({"lat": lat + 1})
-
-        @pl.when(top)
-        def _():
-            greet({"lon": mirror})
-
-        @pl.when(top_far)
-        def _():
-            greet({"lon": mirror_next})
-
-        greet({"lon": east})
-        greet({"lon": west})
+        def when(condition, *steps):
+            @pl.when(condition)
+            def _():
+                for step in steps:
+                    step()
+
+        def both(a, b):
+            return jnp.logical_or(a, b)
+
+        when(has_south, lambda: greet({"lat": lat - 1}))
+        when(has_north, lambda: greet({"lat": lat + 1}))
+        when(mirror_late, lambda: greet({"lon": mirror}))
+        when(both(next_late, next_same), lambda: greet({"lon": mirror_next}))
+        when(jnp.logical_not(early_east), lambda: greet({"lon": east}))
+        when(jnp.logical_not(early_west), lambda: greet({"lon": west}))
 
         body_rows = pl.ds(PAD, rows)
         loads = [
@@ -129,8 +138,19 @@
         slot_of = lane // SLOT
         sl = lane % SLOT
 
-        expected = 2 + has_south.astype(I32) + has_north.astype(I32) + top.astype(I32) + top_far.astype(I32)
-        pl.semaphore_wait(barrier, expected)
+        greetings = (
+            has_south, has_north, mirror_early, both(next_early, next_same),
+            jnp.logical_not(late_west), jnp.logical_not(late_east),
+        )
+        pl.semaphore_wait(barrier, sum(one.astype(I32) for one in greetings))
+
+        def tell(index, device):
+            pl.semaphore_signal(late_ready.at[index], inc=1, device_id=device, device_id_type=MESH)
+
+        when(mirror_early, lambda: tell(0, {"lon": mirror}))
+        when(next_early, lambda: tell(1, {"lon": mirror_next}))
+        when(early_east, lambda: tell(2, {"lon": east}))
+        when(early_west, lambda: tell(3, {"lon": west}))
 
         def remote(src, dst, index, device):
             return pltpu.make_async_remote_copy(
@@ -163,20 +183,9 @@
         eastward = remote(to_e, from_w, 11, {"lon": east})
         westward = remote(to_w, from_e, 12, {"lon": west})
 
-        @pl.when(top)
-        def _():
-            for copy in folded:
-                copy.start()
-
-        @pl.when(has_south)
-        def _():
-            for copy in southward:
-                copy.start()
-
-        @pl.when(has_north)
-        def _():
-            for copy in northward:
-                copy.start()
+        when(mirror_early, *[copy.start for copy in folded])
+        when(has_south, *[copy.start for copy in southward])
+        when(has_north, *[copy.start for copy in northward])
 
         for load in loads[:4]:
             load.wait()
@@ -207,16 +216,10 @@
             to_e[m] = jnp.where(sl < 3, t2, jnp.where(sl < 5, s_up, jnp.where(sl < 6, lanes(u2, 3), n_up)))
             to_w[m] = jnp.where(sl < 3, n_down, jnp.where(sl < 5, t2, s_up))
 
-        @pl.when(top_far)
-        def _():
-            folded_next.start()
-
-        @pl.when(top_self)
-        def _():
-            own_next.start()
-
-        eastward.start()
-        westward.start()
+        when(top_self, own_next.start)
+        when(both(next_early, next_same), folded_next.start)
+        when(jnp.logical_not(late_east), eastward.start)
+        when(jnp.logical_not(late_west), westward.start)
 
         @pl.loop(0, levels)
         def _(k):
@@ -250,8 +253,7 @@
         fy[0, pl.ds(rows, 8)] = jnp.zeros((8, 128), F32)
         fy[1, pl.ds(rows, 8)] = jnp.zeros((8, 128), F32)
 
-        @pl.loop(0, levels)
-        def _(k):
+        def interior(k):
             kp = jnp.minimum(k + 1, levels - 1)
             km = jnp.maximum(k - 1, 0)
             ends = jnp.logical_or(k == 0, k == levels - 1)
@@ -295,6 +297,16 @@
                     fy[i, pl.ds(8 * g, 8)] = f
                     f_north = fy[i, pl.ds(8 * g + 1, 8)]
                     outs[i][k, pl.ds(8 * g, 8)] = jnp.where(here, total[i] + (f - f_north), 0.0)
+
+        pl.loop(0, levels)(interior)
+
+        def heard(index):
+            return lambda: pl.semaphore_wait(late_ready.at[index], 1)
+
+        when(late_east, heard(3), eastward.start)
+        when(late_west, heard(2), westward.start)
+        when(mirror_late, heard(0), *[copy.start for copy in folded])
+        when(next_late, heard(1), folded_next.start)
 
         eastward.wait_recv()
         westward.wait_recv()
@@ -557,6 +569,7 @@
                 pltpu.SemaphoreType.DMA((6,)),
                 pltpu.SemaphoreType.DMA((13,)),
                 pltpu.SemaphoreType.DMA((13,)),
+                pltpu.SemaphoreType.REGULAR((4,)),
             ],
             compiler_params=pltpu.CompilerParams(collective_id=0, has_side_effects=True),
             name="tracer_step",

time: 15.7 us -> 13.8 us (0.88)
  the two profiles are of different devices: /device:TPU:29 before, /device:TPU:28 now
where the time goes in v3:
time: 13.8 us; the launch traced here: 13.6 us
  Pallas kernels  13 us (94%)
  between operations  0.64 us (5%)
    pallas_call x1, Pallas kernels, body(): pl.pallas_call(make_kernel(nlon, nlat, levels, rows), out_shape=(pltpu.VM...  11.9 us
    pallas_call x1, Pallas kernels, body(): pl.pallas_call(make_edge_kernel(levels, rows), out_shape=(plain, plain),...  1.08 us

profile of v3, /device:TPU:28, one launch (start us, length us, event | category | flops | bytes accessed | tf_op | source)
XLA Modules:
  0.0 13.6 jit_solution(16179285086092866711)
XLA Ops:
  0.6 11.9 %tracer_step.1 = (f32[16,32,128]{2,1,0:T(8,128)S(1)}, f32[16,32,128]{2,1,0:T(8,128)S(1)}, f32[2,16,48,128]{3,2,1,0:T(8,128)S(1)}, f32[16,48,128]{2,1,0:T(8,128)S...) custom-call(f32[16,32,128]{2,1,0:T(8,128)} %t_hbm.1, ...), custom_call_target="tpu_custom_call" | custom-call | tf_op jit(solution)/shard_map/tracer_step/pallas_call | solution.py:538
  12.6 1.1 %edge_rows.1 = (f32[16,32,128]{2,1,0:T(8,128)}, f32[16,32,128]{2,1,0:T(8,128)}) custom-call(f32[16,32,128]{2,1,0:T(8,128)S(1)} %get-tuple-element.10.t_part, f32[16,32,128]{2,1,0:T(8,128)S(1)} %get-tuple-element.11.s_part, f32[2,16,48,128]{3,2,1,0:T(8,128)S(1)} %get-tuple-element.12.q, f32[16,48,128]{2,1,0:T(8,128)S(1)} %get-tuple-element.13.v, ...), custom_call_target="tpu_custom_call" | custom-call | tf_op jit(solution)/shard_map/edge_rows/pallas_call | solution.py:577

commit v4 on v3

--- a/solution.py
+++ b/solution.py
@@ -88,6 +88,8 @@
         mirror_far = mirror_next != lon
         top_far = jnp.logical_and(top, mirror_far)
         top_self = jnp.logical_and(top, jnp.logical_not(mirror_far))
+        below_top = lat == nlat - 2
+        plain = jnp.logical_not(top)
         half, quarter = nlon // 2, nlon // 4
         place = lax.rem(lon, half)
         early = place < quarter
@@ -116,7 +118,7 @@
             return jnp.logical_or(a, b)
 
         when(has_south, lambda: greet({"lat": lat - 1}))
-        when(has_north, lambda: greet({"lat": lat + 1}))
+        when(jnp.logical_and(has_north, jnp.logical_not(below_top)), lambda: greet({"lat": lat + 1}))
         when(mirror_late, lambda: greet({"lon": mirror}))
         when(both(next_late, next_same), lambda: greet({"lon": mirror_next}))
         when(jnp.logical_not(early_east), lambda: greet({"lon": east}))
@@ -139,18 +141,17 @@
         sl = lane % SLOT
 
         greetings = (
-            has_south, has_north, mirror_early, both(next_early, next_same),
+            jnp.logical_and(has_south, plain), has_north, mirror_early, both(next_early, next_same),
             jnp.logical_not(late_west), jnp.logical_not(late_east),
         )
-        pl.semaphore_wait(barrier, sum(one.astype(I32) for one in greetings))
+
+        def meet():
+            pl.semaphore_wait(barrier, sum(one.astype(I32) for one in greetings))
 
         def tell(index, device):
-            pl.semaphore_signal(late_ready.at[index], inc=1, device_id=device, device_id_type=MESH)
-
-        when(mirror_early, lambda: tell(0, {"lon": mirror}))
-        when(next_early, lambda: tell(1, {"lon": mirror_next}))
-        when(early_east, lambda: tell(2, {"lon": east}))
-        when(early_west, lambda: tell(3, {"lon": west}))
+            return lambda: pl.semaphore_signal(
+                late_ready.at[index], inc=1, device_id=device, device_id_type=MESH
+            )
 
         def remote(src, dst, index, device):
             return pltpu.make_async_remote_copy(
@@ -183,9 +184,13 @@
         eastward = remote(to_e, from_w, 11, {"lon": east})
         westward = remote(to_w, from_e, 12, {"lon": west})
 
-        when(mirror_early, *[copy.start for copy in folded])
-        when(has_south, *[copy.start for copy in southward])
-        when(has_north, *[copy.start for copy in northward])
+        @pl.when(top)
+        def _():
+            meet()
+            when(mirror_early, *[copy.start for copy in folded], tell(0, {"lon": mirror}))
+            when(next_early, tell(1, {"lon": mirror_next}))
+            when(early_east, tell(2, {"lon": east}))
+            when(early_west, tell(3, {"lon": west}))
 
         for load in loads[:4]:
             load.wait()
@@ -217,9 +222,14 @@
             to_w[m] = jnp.where(sl < 3, n_down, jnp.where(sl < 5, t2, s_up))
 
         when(top_self, own_next.start)
-        when(both(next_early, next_same), folded_next.start)
-        when(jnp.logical_not(late_east), eastward.start)
-        when(jnp.logical_not(late_west), westward.start)
+        def send_columns():
+            when(jnp.logical_not(late_east), eastward.start)
+            when(jnp.logical_not(late_west), westward.start)
+
+        @pl.when(top)
+        def _():
+            when(both(next_early, next_same), folded_next.start)
+            send_columns()
 
         @pl.loop(0, levels)
         def _(k):
@@ -248,6 +258,16 @@
         face_y[pl.ds(0, 8)] = pad_n
         face_y[pl.ds(top_row, 8)] = pad_n
 
+        @pl.when(plain)
+        def _():
+            meet()
+            send_columns()
+            when(early_east, tell(2, {"lon": east}))
+            when(early_west, tell(3, {"lon": west}))
+            when(below_top, tell(4, {"lat": lat + 1}))
+            when(has_south, *[copy.start for copy in southward])
+            when(has_north, *[copy.start for copy in northward])
+
         outs = (t_out, s_out)
         loads[4].wait()
         fy[0, pl.ds(rows, 8)] = jnp.zeros((8, 128), F32)
@@ -298,15 +318,73 @@
                     f_north = fy[i, pl.ds(8 * g + 1, 8)]
                     outs[i][k, pl.ds(8 * g, 8)] = jnp.where(here, total[i] + (f - f_north), 0.0)
 
-        pl.loop(0, levels)(interior)
-
         def heard(index):
             return lambda: pl.semaphore_wait(late_ready.at[index], 1)
+
+        pl.loop(0, levels // 2)(interior)
+        when(top, heard(4), *[copy.start for copy in southward])
+        pl.loop(levels // 2, levels)(interior)
 
         when(late_east, heard(3), eastward.start)
         when(late_west, heard(2), westward.start)
         when(mirror_late, heard(0), *[copy.start for copy in folded])
         when(next_late, heard(1), folded_next.start)
+
+        def edge_rows():
+            @pl.when(jnp.logical_not(has_south))
+            def _():
+                hn[lo] = jnp.zeros((2, 128), I32)
+
+                @pl.loop(0, levels)
+                def _(k):
+                    h[0, k, lo] = jnp.zeros((2, 128), F32)
+                    h[1, k, lo] = jnp.zeros((2, 128), F32)
+                    hv[k, lo] = jnp.zeros((2, 128), F32)
+
+            @pl.when(has_south)
+            def _():
+                for copy in northward:
+                    copy.wait_recv()
+
+            @pl.when(has_north)
+            def _():
+                for copy in southward:
+                    copy.wait_recv()
+
+            @pl.when(top)
+            def _():
+                for copy in folded:
+                    copy.wait_recv()
+
+            @pl.when(top_far)
+            def _():
+                folded_next.wait_recv()
+
+            @pl.when(top_self)
+            def _():
+                own_next.wait()
+
+            @pl.when(top)
+            def _():
+                order = lax.rem(128 - lane, 128)
+
+                def mirrored(x):
+                    x = jnp.where(row == 6, rows_by(x, -1), rows_by(x, 1))
+                    return jnp.take_along_axis(x, order, axis=1)
+
+                spot = SLOT * (groups - 1) + MID
+                x = jnp.where(lane == 0, lanes(fb[0], -(spot - 2)), fan[...].astype(F32))
+                hn[hi] = mirrored(x)[6:8].astype(I32)
+
+                @pl.loop(0, packs)
+                def _(m):
+                    for part in range(16 // groups):
+                        k = packs * part + m
+                        for i in range(2):
+                            x = jnp.where(lane == 0, lanes(fb[m], -(span * part + spot + 2 * i)), fa[i, k])
+                            h[i, k, hi] = mirrored(x)[6:8]
+
+        when(late_west, edge_rows)
 
         eastward.wait_recv()
         westward.wait_recv()
@@ -356,72 +434,20 @@
                 d = jnp.where(wet, qb - qa, 0.0)
                 f = tracer_flux(keep, c, up, coef, sk, qa, qb, d, lanes(d, 1), lanes(d, -1), zsum_of(sums[i], m))
                 change = f - lanes(f, -1)
-                ex[i, m] = jnp.where(sl < MID, lanes(change, -3), lanes(change, 2))
+                change = jnp.where(sl < MID, lanes(change, -3), lanes(change, 2))
+                ex[i, m] = jnp.where(level.astype(F32) < px[2 * packs], change, 0.0)
 
         ends_x = jnp.logical_or(lane < 2, lane > 125)
 
-        @pl.loop(0, packs)
-        def _(m):
+        for m in range(packs):
             for i in range(2):
                 packed = ex[i, m]
                 for slot in range(16):
                     k = packs * (slot // groups) + m
                     at = pl.ds(8 * (slot % groups), 8)
-                    here = jnp.logical_and(ends_x, k < n[pl.ds(PAD + 8 * (slot % groups), 8)])
-                    outs[i][k, at] = outs[i][k, at] + jnp.where(here, lanes(packed, -(SLOT * slot + MID)), 0.0)
-
-        @pl.when(jnp.logical_not(has_south))
-        def _():
-            hn[lo] = jnp.zeros((2, 128), I32)
-
-            @pl.loop(0, levels)
-            def _(k):
-                h[0, k, lo] = jnp.zeros((2, 128), F32)
-                h[1, k, lo] = jnp.zeros((2, 128), F32)
-                hv[k, lo] = jnp.zeros((2, 128), F32)
-
-        @pl.when(has_south)
-        def _():
-            for copy in northward:
-                copy.wait_recv()
-
-        @pl.when(has_north)
-        def _():
-            for copy in southward:
-                copy.wait_recv()
-
-        @pl.when(top)
-        def _():
-            for copy in folded:
-                copy.wait_recv()
-
-        @pl.when(top_far)
-        def _():
-            folded_next.wait_recv()
-
-        @pl.when(top_self)
-        def _():
-            own_next.wait()
-
-        @pl.when(top)
-        def _():
-            order = lax.rem(128 - lane, 128)
-
-            def mirrored(x):
-                x = jnp.where(row == 6, rows_by(x, -1), rows_by(x, 1))
-                return jnp.take_along_axis(x, order, axis=1)
-
-            spot = SLOT * (groups - 1) + MID
-            x = jnp.where(lane == 0, lanes(fb[0], -(spot - 2)), fan[...].astype(F32))
-            hn[hi] = mirrored(x)[6:8].astype(I32)
-
-            @pl.loop(0, packs)
-            def _(m):
-                for part in range(16 // groups):
-                    k = packs * part + m
-                    for i in range(2):
-                        x = jnp.where(lane == 0, lanes(fb[m], -(span * part + spot + 2 * i)), fa[i, k])
-                        h[i, k, hi] = mirrored(x)[6:8]
+                    outs[i][k, at] = outs[i][k, at] + jnp.where(ends_x, lanes(packed, -(SLOT * slot + MID)), 0.0)
+
+        when(jnp.logical_not(late_west), edge_rows)
 
         eastward.wait_send()
         westward.wait_send()
@@ -450,14 +476,14 @@
 
 def make_edge_kernel(levels, rows):
     top_row = PAD + rows
-    unroll = 4
-
-    def kernel(t_part, s_part, q, v, n, h, hv, hn, t_out, s_out, ey, done, sem):
+    pieces = 2
+
+    def kernel(t_part, s_part, q, v, n, h, hv, hn, t_out, s_out, done, sem, end_sem):
         parts = (t_part, s_part)
         outs = (t_out, s_out)
         row = lax.broadcasted_iota(I32, (8, 128), 0)
         inner = pl.ds(8, rows - 16)
-        south, north = pl.ds(0, 8), pl.ds(rows - 8, 8)
+        ends = (pl.ds(0, 8), pl.ds(rows - 8, 8))
         stores = [
             pltpu.make_async_copy(parts[i].at[:, inner], outs[i].at[:, inner], sem.at[i]) for i in range(2)
         ]
@@ -476,51 +502,42 @@
         na, nb = edge_pair(hn[...], lambda at: n[pl.ds(at, 8)])
         face_n = jnp.minimum(na, nb)
         used = jnp.logical_or(jnp.logical_or(row == 1, row == 2), jnp.logical_or(row == 5, row == 6))
-
-        @pl.loop(0, levels // unroll)
-        def _(block):
-            for j in range(unroll):
-                k = block * unroll + j
-                z = TOTAL_DEPTH * (k.astype(F32) + 0.5) / levels
-                pair = [edge_pair(h[i, k], lambda at, i=i: q[i, k, pl.ds(at, 8)]) for i in range(2)]
-                ra, rb = [density(pair[0][j], pair[1][j], z) for j in range(2)]
+        keep_n = jnp.where(used, face_n, 0)
+        cell_n = (jnp.where(row < 2, n[pl.ds(PAD, 8)], 0), jnp.where(row > 5, n[pl.ds(top_row - 8, 8)], 0))
+
+        def level(k):
+            pair = [edge_pair(h[i, k], lambda at, i=i: q[i, k, pl.ds(at, 8)]) for i in range(2)]
+            ra, rb = [density(pair[0][j], pair[1][j], TOTAL_DEPTH * (k + 0.5) / levels) for j in range(2)]
+            return pair, [pair[0][0] + pair[0][1], pair[1][0] + pair[1][1], ra + rb], rb - ra
+
+        held = [level(0), level(1)]
+        for k in range(levels):
+            below, above = held[max(k - 1, 0)][1], held[min(k + 1, levels - 1)][1]
+            pair, _, rho_diff = held[k]
+            half_scale = 0.5 if k in (0, levels - 1) else 0.25
+            wet, keep = k < face_n, k < keep_n
+            c = jnp.where(row < 2, hv[k], jnp.where(row < 4, v[k, pl.ds(PAD - 2, 8)], v[k, pl.ds(top_row - 7, 8)]))
+            up, coef = courant_terms(c)
+            sk = slope_term(rho_diff, above[2] - below[2], half_scale)
+            for i in range(2):
+                qa, qb = pair[i]
+                d = jnp.where(wet, qb - qa, 0.0)
+                f = tracer_flux(keep, c, up, coef, sk, qa, qb, d, rows_by(d, 1), rows_by(d, -1), above[i] - below[i])
+                change = f - rows_by(f, -1)
+                for e, shift in enumerate((-1, 2)):
+                    done[2 * i + e, k] = parts[i][k, ends[e]] + jnp.where(k < cell_n[e], rows_by(change, shift), 0.0)
+            if k + 2 < levels:
+                held.append(level(k + 2))
+            if (k + 1) % (levels // pieces) == 0:
+                some = pl.ds(k + 1 - levels // pieces, levels // pieces)
                 for i in range(2):
-                    ey[2 * i, k] = pair[i][0]
-                    ey[2 * i + 1, k] = pair[i][1]
-                    ey[4 + i, k] = pair[i][0] + pair[i][1]
-                ey[6, k] = ra + rb
-                ey[7, k] = rb - ra
-
-        n_south = jnp.where(row < 2, n[pl.ds(PAD, 8)], 0)
-        n_north = jnp.where(row > 5, n[pl.ds(top_row - 8, 8)], 0)
-
-        @pl.loop(0, levels // unroll)
-        def _(block):
-            for j in range(unroll):
-                k = block * unroll + j
-                kp = jnp.minimum(k + 1, levels - 1)
-                km = jnp.maximum(k - 1, 0)
-                ends = jnp.logical_or(k == 0, k == levels - 1)
-                half_scale = jnp.where(ends, 0.5, 0.25).astype(F32)
-                wet = k < face_n
-                keep = jnp.logical_and(wet, used)
-                c = jnp.where(row < 2, hv[k], jnp.where(row < 4, v[k, pl.ds(PAD - 2, 8)], v[k, pl.ds(top_row - 7, 8)]))
-                up, coef = courant_terms(c)
-                sk = slope_term(ey[7, k], ey[6, kp] - ey[6, km], half_scale)
-                for i in range(2):
-                    qa, qb = ey[2 * i, k], ey[2 * i + 1, k]
-                    d = jnp.where(wet, qb - qa, 0.0)
-                    zsum = ey[4 + i, kp] - ey[4 + i, km]
-                    f = tracer_flux(keep, c, up, coef, sk, qa, qb, d, rows_by(d, 1), rows_by(d, -1), zsum)
-                    change = f - rows_by(f, -1)
-                    done[2 * i, k] = parts[i][k, south] + jnp.where(k < n_south, rows_by(change, -1), 0.0)
-                    done[2 * i + 1, k] = parts[i][k, north] + jnp.where(k < n_north, rows_by(change, 2), 0.0)
-
-        for i in range(2):
-            stores.append(pltpu.make_async_copy(done.at[2 * i], outs[i].at[:, south], sem.at[2 + 2 * i]))
-            stores.append(pltpu.make_async_copy(done.at[2 * i + 1], outs[i].at[:, north], sem.at[3 + 2 * i]))
-        for store in stores[2:]:
-            store.start()
+                    for e in range(2):
+                        piece = pltpu.make_async_copy(
+                            done.at[2 * i + e, some], outs[i].at[some, ends[e]],
+                            end_sem.at[2 * i + e, k // (levels // pieces)],
+                        )
+                        piece.start()
+                        stores.append(piece)
         for store in stores:
             store.wait()
 
@@ -569,7 +586,7 @@
                 pltpu.SemaphoreType.DMA((6,)),
                 pltpu.SemaphoreType.DMA((13,)),
                 pltpu.SemaphoreType.DMA((13,)),
-                pltpu.SemaphoreType.REGULAR((4,)),
+                pltpu.SemaphoreType.REGULAR((5,)),
             ],
             compiler_params=pltpu.CompilerParams(collective_id=0, has_side_effects=True),
             name="tracer_step",
@@ -580,9 +597,9 @@
             in_specs=[pl.BlockSpec(memory_space=pltpu.VMEM)] * 8,
             out_specs=(pl.BlockSpec(memory_space=pl.ANY),) * 2,
             scratch_shapes=[
-                pltpu.VMEM((8, levels, 8, cols), F32),
                 pltpu.VMEM((4, levels, 8, cols), F32),
-                pltpu.SemaphoreType.DMA((6,)),
+                pltpu.SemaphoreType.DMA((2,)),
+                pltpu.SemaphoreType.DMA((4, 2)),
             ],
             name="edge_rows",
         )(*[pltpu.with_memory_space_constraint(part, pltpu.VMEM) for part in parts])

time: 13.8 us -> 13.1 us (0.949)
  Pallas kernels: 13 us -> 12.3 us
    pallas_call x1, Pallas kernels: 11.9 us -> 11.3 us  [body(): pl.pallas_call(make_kernel(nlon, nlat, levels, rows), out_shape=(pltpu.VM...]
where the time goes in v4:
time: 13.1 us; the launch traced here: 12.9 us
  Pallas kernels  12.3 us (94%)
  between operations  0.64 us (5%)
    pallas_call x1, Pallas kernels, body(): pl.pallas_call(make_kernel(nlon, nlat, levels, rows), out_shape=(pltpu.VM...  11.3 us
    pallas_call x1, Pallas kernels, body(): pl.pallas_call(make_edge_kernel(levels, rows), out_shape=(plain, plain),...  0.99 us

profile of v4, /device:TPU:28, one launch (start us, length us, event | category | flops | bytes accessed | tf_op | source)
XLA Modules:
  0.0 12.9 jit_solution(9105968964975966278)
XLA Ops:
  0.6 11.3 %tracer_step.1 = (f32[16,32,128]{2,1,0:T(8,128)S(1)}, f32[16,32,128]{2,1,0:T(8,128)S(1)}, f32[2,16,48,128]{3,2,1,0:T(8,128)S(1)}, f32[16,48,128]{2,1,0:T(8,128)S...) custom-call(f32[16,32,128]{2,1,0:T(8,128)} %t_hbm.1, ...), custom_call_target="tpu_custom_call" | custom-call | tf_op jit(solution)/shard_map/tracer_step/pallas_call | solution.py:555
  11.9 1.0 %edge_rows.1 = (f32[16,32,128]{2,1,0:T(8,128)}, f32[16,32,128]{2,1,0:T(8,128)}) custom-call(f32[16,32,128]{2,1,0:T(8,128)S(1)} %get-tuple-element.10.t_part, f32[16,32,128]{2,1,0:T(8,128)S(1)} %get-tuple-element.11.s_part, f32[2,16,48,128]{3,2,1,0:T(8,128)S(1)} %get-tuple-element.12.q, f32[16,48,128]{2,1,0:T(8,128)S(1)} %get-tuple-element.13.v, ...), custom_call_target="tpu_custom_call" | custom-call | tf_op jit(solution)/shard_map/edge_rows/pallas_call | solution.py:594

commit v5 on v4

--- a/solution.py
+++ b/solution.py
@@ -59,6 +59,63 @@
     return pltpu.roll(x, shift % 8, axis=x.ndim - 2)
 
 
+def edge_rows(north, q, v, n, halo, halo_v, halo_n, levels, rows, emit):
+    top_row = PAD + rows
+    hop = levels // 2
+    row = lax.broadcasted_iota(I32, (8, 128), 0)
+    low, place = row < 4, row % 4
+
+    def own(load, m, base):
+        return jnp.where(low, load(m, base), load(m + hop, base - 4))
+
+    def pair(halo, load, m):
+        if north:
+            a = jnp.where(place == 3, rows_by(halo, 1), own(load, m, top_row - 3))
+            b = jnp.where(place > 1, halo, own(load, m, top_row - 2))
+        else:
+            a = jnp.where(place < 2, halo, own(load, m, PAD - 2))
+            b = jnp.where(place < 1, rows_by(halo, -1), own(load, m, PAD - 1))
+        return a, b
+
+    def load_v(k, base):
+        return v[k, pl.ds(base, 8)]
+
+    face_n = jnp.minimum(*pair(halo_n, lambda k, base: n[pl.ds(base, 8)], 0))
+    keep_n = jnp.where(jnp.logical_or(place == 1, place == 2), face_n, 0)
+
+    def level(m):
+        z = jnp.where(low, TOTAL_DEPTH * (m + 0.5) / levels, TOTAL_DEPTH * (m + hop + 0.5) / levels)
+        t, s = [pair(halo(i, m), lambda k, base, i=i: q[i, k, pl.ds(base, 8)], m) for i in range(2)]
+        ra, rb = [density(t[j], s[j], z) for j in range(2)]
+        return (t, s), (t[0] + t[1], s[0] + s[1], ra + rb), rb - ra
+
+    held = [level(m) for m in range(hop)]
+    for m in range(hop):
+        tracers, sums, rho_diff = held[m]
+        zsums = []
+        for j in range(3):
+            above = held[m + 1][1][j] if m + 1 < hop else jnp.where(low, rows_by(held[0][1][j], 4), sums[j])
+            below = held[m - 1][1][j] if m > 0 else jnp.where(low, sums[j], rows_by(held[hop - 1][1][j], 4))
+            zsums.append(above - below)
+        half_scale = 0.25
+        if m == 0:
+            half_scale = jnp.where(low, 0.5, 0.25)
+        if m == hop - 1:
+            half_scale = jnp.where(low, 0.25, 0.5)
+        k = jnp.where(low, m, m + hop)
+        wet, keep = k < face_n, k < keep_n
+        c = own(load_v, m, top_row - 3) if north else jnp.where(place < 2, halo_v(m), own(load_v, m, PAD - 2))
+        up, coef = courant_terms(c)
+        sk = slope_term(rho_diff, zsums[2], half_scale)
+        for i in range(2):
+            qa, qb = tracers[i]
+            d = jnp.where(wet, qb - qa, 0.0)
+            f = tracer_flux(keep, c, up, coef, sk, qa, qb, d, rows_by(d, 1), rows_by(d, -1), zsums[i])
+            change = f - rows_by(f, -1)
+            emit(i, m, rows_by(change, 6 if north else -1))
+            emit(i, m + hop, rows_by(change, 2 if north else 3))
+
+
 def make_kernel(nlon, nlat, levels, rows):
     groups = rows // 8
     per = 16 // groups
@@ -71,8 +128,8 @@
 
     def kernel(
         t_hbm, s_hbm, u_hbm, v_hbm, n_hbm,
-        t_out, s_out, q, v, n, h, hv, hn,
-        rho, u, face_x, keep_x, face_y, keep_y, fy,
+        t_out, s_out, q, v, n, hp, hn,
+        h, hv, hs, h_north, hs_north, rho, u, face_x, keep_x, face_y, keep_y, fy,
         px, to_e, to_w, from_w, from_e, fa, fb, fan, ex,
         load_sem, send_sem, recv_sem, late_ready,
     ):
@@ -167,12 +224,12 @@
             remote(t_hbm.at[:, last], h.at[0, :, lo], 0, {"lat": lat + 1}),
             remote(s_hbm.at[:, last], h.at[1, :, lo], 1, {"lat": lat + 1}),
             remote(v_hbm.at[:, pl.ds(rows - 1, 1)], hv.at[:, pl.ds(1, 1)], 2, {"lat": lat + 1}),
-            remote(n_hbm.at[last], hn.at[lo], 3, {"lat": lat + 1}),
+            remote(n_hbm.at[last], hs.at[lo], 3, {"lat": lat + 1}),
         ]
         southward = [
-            remote(t_hbm.at[:, first], h.at[0, :, hi], 4, {"lat": lat - 1}),
-            remote(s_hbm.at[:, first], h.at[1, :, hi], 5, {"lat": lat - 1}),
-            remote(n_hbm.at[first], hn.at[hi], 6, {"lat": lat - 1}),
+            remote(t_hbm.at[:, first], h_north.at[0, :, hi], 4, {"lat": lat - 1}),
+            remote(s_hbm.at[:, first], h_north.at[1, :, hi], 5, {"lat": lat - 1}),
+            remote(n_hbm.at[first], hs_north.at[hi], 6, {"lat": lat - 1}),
         ]
         folded = [
             remote(t_hbm.at[:, fold], fa.at[0, :, hi], 7, {"lon": mirror}),
@@ -330,61 +387,67 @@
         when(mirror_late, heard(0), *[copy.start for copy in folded])
         when(next_late, heard(1), folded_next.start)
 
-        def edge_rows():
-            @pl.when(jnp.logical_not(has_south))
-            def _():
-                hn[lo] = jnp.zeros((2, 128), I32)
-
-                @pl.loop(0, levels)
-                def _(k):
-                    h[0, k, lo] = jnp.zeros((2, 128), F32)
-                    h[1, k, lo] = jnp.zeros((2, 128), F32)
-                    hv[k, lo] = jnp.zeros((2, 128), F32)
-
-            @pl.when(has_south)
-            def _():
-                for copy in northward:
-                    copy.wait_recv()
+        hop = levels // 2
+        low = row < 4
+
+        @pl.when(jnp.logical_not(has_south))
+        def _():
+            hs[lo] = jnp.zeros((2, 128), I32)
+
+            @pl.loop(0, levels)
+            def _(k):
+                h[0, k, lo] = jnp.zeros((2, 128), F32)
+                h[1, k, lo] = jnp.zeros((2, 128), F32)
+                hv[k, lo] = jnp.zeros((2, 128), F32)
+
+        when(has_south, *[copy.wait_recv for copy in northward])
+        cells = jnp.where(row < 2, n[pl.ds(PAD, 8)], 0)
+
+        def put(i, k, change):
+            outs[i][k, pl.ds(0, 8)] = outs[i][k, pl.ds(0, 8)] + jnp.where(k < cells, change, 0.0)
+
+        edge_rows(
+            False, q, v, n,
+            lambda i, m: jnp.where(low, h[i, m], rows_by(h[i, m + hop], 4)),
+            lambda m: jnp.where(low, hv[m], rows_by(hv[m + hop], 4)),
+            jnp.where(low, hs[...], rows_by(hs[...], 4)),
+            levels, rows, put,
+        )
+
+        def north_rows():
+            when(has_north, *[copy.wait_recv for copy in southward])
+            when(top, *[copy.wait_recv for copy in folded])
+            when(top_far, folded_next.wait_recv)
+            when(top_self, own_next.wait)
 
             @pl.when(has_north)
             def _():
-                for copy in southward:
-                    copy.wait_recv()
-
-            @pl.when(top)
-            def _():
-                for copy in folded:
-                    copy.wait_recv()
-
-            @pl.when(top_far)
-            def _():
-                folded_next.wait_recv()
-
-            @pl.when(top_self)
-            def _():
-                own_next.wait()
+                hn[...] = jnp.where(low, rows_by(hs_north[...], -4), hs_north[...])
+                for m in range(hop):
+                    for i in range(2):
+                        hp[i, m] = jnp.where(low, rows_by(h_north[i, m], -4), h_north[i, m + hop])
 
             @pl.when(top)
             def _():
                 order = lax.rem(128 - lane, 128)
+                spot = SLOT * (groups - 1) + MID
 
                 def mirrored(x):
-                    x = jnp.where(row == 6, rows_by(x, -1), rows_by(x, 1))
+                    x = jnp.where(row % 2 == 0, rows_by(x, -1), rows_by(x, 1))
                     return jnp.take_along_axis(x, order, axis=1)
 
-                spot = SLOT * (groups - 1) + MID
                 x = jnp.where(lane == 0, lanes(fb[0], -(spot - 2)), fan[...].astype(F32))
-                hn[hi] = mirrored(x)[6:8].astype(I32)
-
-                @pl.loop(0, packs)
-                def _(m):
-                    for part in range(16 // groups):
+                hn[...] = mirrored(jnp.where(low, rows_by(x, -4), x)).astype(I32)
+                for m in range(packs):
+                    next_cells = jnp.where(low, rows_by(fb[m], -4), lanes(fb[m], -span * (hop // packs)))
+                    for part in range(hop // packs):
                         k = packs * part + m
                         for i in range(2):
-                            x = jnp.where(lane == 0, lanes(fb[m], -(span * part + spot + 2 * i)), fa[i, k])
-                            h[i, k, hi] = mirrored(x)[6:8]
-
-        when(late_west, edge_rows)
+                            x = jnp.where(low, rows_by(fa[i, k], -4), fa[i, k + hop])
+                            x = jnp.where(lane == 0, lanes(next_cells, -(span * part + spot + 2 * i)), x)
+                            hp[i, k] = mirrored(x)
+
+        when(late_west, north_rows)
 
         eastward.wait_recv()
         westward.wait_recv()
@@ -447,7 +510,7 @@
                     at = pl.ds(8 * (slot % groups), 8)
                     outs[i][k, at] = outs[i][k, at] + jnp.where(ends_x, lanes(packed, -(SLOT * slot + MID)), 0.0)
 
-        when(jnp.logical_not(late_west), edge_rows)
+        when(jnp.logical_not(late_west), north_rows)
 
         eastward.wait_send()
         westward.wait_send()
@@ -476,69 +539,27 @@
 
 def make_edge_kernel(levels, rows):
     top_row = PAD + rows
-    pieces = 2
-
-    def kernel(t_part, s_part, q, v, n, h, hv, hn, t_out, s_out, done, sem, end_sem):
+
+    def kernel(t_part, s_part, q, v, n, hp, hn, t_out, s_out, done, sem, end_sem):
         parts = (t_part, s_part)
         outs = (t_out, s_out)
         row = lax.broadcasted_iota(I32, (8, 128), 0)
-        inner = pl.ds(8, rows - 16)
-        ends = (pl.ds(0, 8), pl.ds(rows - 8, 8))
-        stores = [
-            pltpu.make_async_copy(parts[i].at[:, inner], outs[i].at[:, inner], sem.at[i]) for i in range(2)
-        ]
+        rest, end = pl.ds(0, rows - 8), pl.ds(rows - 8, 8)
+        stores = [pltpu.make_async_copy(parts[i].at[:, rest], outs[i].at[:, rest], sem.at[i]) for i in range(2)]
         for store in stores:
             store.start()
 
-        def edge_pair(halo, load):
-            a = jnp.where(
-                row < 2, halo, jnp.where(row < 4, load(PAD - 2), jnp.where(row < 7, load(top_row - 7), rows_by(halo, 1)))
-            )
-            b = jnp.where(
-                row < 1, rows_by(halo, -1), jnp.where(row < 4, load(PAD - 1), jnp.where(row < 6, load(top_row - 6), halo))
-            )
-            return a, b
-
-        na, nb = edge_pair(hn[...], lambda at: n[pl.ds(at, 8)])
-        face_n = jnp.minimum(na, nb)
-        used = jnp.logical_or(jnp.logical_or(row == 1, row == 2), jnp.logical_or(row == 5, row == 6))
-        keep_n = jnp.where(used, face_n, 0)
-        cell_n = (jnp.where(row < 2, n[pl.ds(PAD, 8)], 0), jnp.where(row > 5, n[pl.ds(top_row - 8, 8)], 0))
-
-        def level(k):
-            pair = [edge_pair(h[i, k], lambda at, i=i: q[i, k, pl.ds(at, 8)]) for i in range(2)]
-            ra, rb = [density(pair[0][j], pair[1][j], TOTAL_DEPTH * (k + 0.5) / levels) for j in range(2)]
-            return pair, [pair[0][0] + pair[0][1], pair[1][0] + pair[1][1], ra + rb], rb - ra
-
-        held = [level(0), level(1)]
-        for k in range(levels):
-            below, above = held[max(k - 1, 0)][1], held[min(k + 1, levels - 1)][1]
-            pair, _, rho_diff = held[k]
-            half_scale = 0.5 if k in (0, levels - 1) else 0.25
-            wet, keep = k < face_n, k < keep_n
-            c = jnp.where(row < 2, hv[k], jnp.where(row < 4, v[k, pl.ds(PAD - 2, 8)], v[k, pl.ds(top_row - 7, 8)]))
-            up, coef = courant_terms(c)
-            sk = slope_term(rho_diff, above[2] - below[2], half_scale)
-            for i in range(2):
-                qa, qb = pair[i]
-                d = jnp.where(wet, qb - qa, 0.0)
-                f = tracer_flux(keep, c, up, coef, sk, qa, qb, d, rows_by(d, 1), rows_by(d, -1), above[i] - below[i])
-                change = f - rows_by(f, -1)
-                for e, shift in enumerate((-1, 2)):
-                    done[2 * i + e, k] = parts[i][k, ends[e]] + jnp.where(k < cell_n[e], rows_by(change, shift), 0.0)
-            if k + 2 < levels:
-                held.append(level(k + 2))
-            if (k + 1) % (levels // pieces) == 0:
-                some = pl.ds(k + 1 - levels // pieces, levels // pieces)
-                for i in range(2):
-                    for e in range(2):
-                        piece = pltpu.make_async_copy(
-                            done.at[2 * i + e, some], outs[i].at[some, ends[e]],
-                            end_sem.at[2 * i + e, k // (levels // pieces)],
-                        )
-                        piece.start()
-                        stores.append(piece)
-        for store in stores:
+        cells = jnp.where(row > 5, n[pl.ds(top_row - 8, 8)], 0)
+
+        def put(i, k, change):
+            done[i, k] = parts[i][k, end] + jnp.where(k < cells, change, 0.0)
+
+        edge_rows(True, q, v, n, lambda i, m: hp[i, m], None, hn[...], levels, rows, put)
+
+        ends = [pltpu.make_async_copy(done.at[i], outs[i].at[:, end], end_sem.at[i]) for i in range(2)]
+        for store in ends:
+            store.start()
+        for store in stores + ends:
             store.wait()
 
     return kernel
@@ -560,13 +581,17 @@
                 pltpu.VMEM((2, levels, tall, cols), F32),
                 pltpu.VMEM((levels, tall, cols), F32),
                 pltpu.VMEM((tall, cols), I32),
+                pltpu.VMEM((2, levels // 2, 8, cols), F32),
+                pltpu.VMEM((8, cols), I32),
+            ),
+            in_specs=[pl.BlockSpec(memory_space=pl.ANY)] * 5,
+            out_specs=(pl.BlockSpec(memory_space=pltpu.VMEM),) * 7,
+            scratch_shapes=[
                 pltpu.VMEM((2, levels, 8, cols), F32),
                 pltpu.VMEM((levels, 8, cols), F32),
                 pltpu.VMEM((8, cols), I32),
-            ),
-            in_specs=[pl.BlockSpec(memory_space=pl.ANY)] * 5,
-            out_specs=(pl.BlockSpec(memory_space=pltpu.VMEM),) * 8,
-            scratch_shapes=[
+                pltpu.VMEM((2, levels, 8, cols), F32),
+                pltpu.VMEM((8, cols), I32),
                 pltpu.VMEM((levels, tall, cols), F32),
                 pltpu.VMEM((levels, rows, cols), F32),
                 pltpu.VMEM((rows, cols), I32),
@@ -594,12 +619,12 @@
         return pl.pallas_call(
             make_edge_kernel(levels, rows),
             out_shape=(plain, plain),
-            in_specs=[pl.BlockSpec(memory_space=pltpu.VMEM)] * 8,
+            in_specs=[pl.BlockSpec(memory_space=pltpu.VMEM)] * 7,
             out_specs=(pl.BlockSpec(memory_space=pl.ANY),) * 2,
             scratch_shapes=[
-                pltpu.VMEM((4, levels, 8, cols), F32),
+                pltpu.VMEM((2, levels, 8, cols), F32),
                 pltpu.SemaphoreType.DMA((2,)),
-                pltpu.SemaphoreType.DMA((4, 2)),
+                pltpu.SemaphoreType.DMA((2,)),
             ],
             name="edge_rows",
         )(*[pltpu.with_memory_space_constraint(part, pltpu.VMEM) for part in parts])

time: 13.1 us -> 12.9 us (0.985)
  Pallas kernels: 12.3 us -> 12.1 us
    pallas_call x1, Pallas kernels: 0.99 us -> 0.82 us  [body(): pl.pallas_call(make_edge_kernel(levels, rows), out_shape=(plain, plain),...]
where the time goes in v5:
time: 12.9 us; the launch traced here: 12.8 us
  Pallas kernels  12.1 us (94%)
  between operations  0.64 us (5%)
    pallas_call x1, Pallas kernels, body(): pl.pallas_call(make_kernel(nlon, nlat, levels, rows), out_shape=(pltpu.VM...  11.3 us
    pallas_call x1, Pallas kernels, body(): pl.pallas_call(make_edge_kernel(levels, rows), out_shape=(plain, plain),...  0.82 us

profile of v5, /device:TPU:28, one launch (start us, length us, event | category | flops | bytes accessed | tf_op | source)
XLA Modules:
  0.0 12.8 jit_solution(7825100975962327988)
XLA Ops:
  0.6 11.3 %tracer_step.1 = (f32[16,32,128]{2,1,0:T(8,128)S(1)}, f32[16,32,128]{2,1,0:T(8,128)S(1)}, f32[2,16,48,128]{3,2,1,0:T(8,128)S(1)}, f32[16,48,128]{2,1,0:T(8,128)S...) custom-call(f32[16,32,128]{2,1,0:T(8,128)} %t_hbm.1, f32[16,32,128]{2,1,0:T(8,128)} %s_hbm.1, ...), custom_call_target="tpu_custom_call" | custom-call | tf_op jit(solution)/shard_map/tracer_step/pallas_call | solution.py:576
  11.9 0.8 %edge_rows.1 = (f32[16,32,128]{2,1,0:T(8,128)}, f32[16,32,128]{2,1,0:T(8,128)}) custom-call(f32[16,32,128]{2,1,0:T(8,128)S(1)} %get-tuple-element.9.t_part, f32[16,32,128]{2,1,0:T(8,128)S(1)} %get-tuple-element.10.s_part, f32[2,16,48,128]{3,2,1,0:T(8,128)S(1)} %get-tuple-element.11.q, f32[16,48,128]{2,1,0:T(8,128)S(1)} %get-tuple-element.12.v, ...), custom_call_target="tpu_custom_call" | custom-call | tf_op jit(solution)/shard_map/edge_rows/pallas_call | solution.py:619

commit v6 on v5

--- a/solution.py
+++ b/solution.py
@@ -288,6 +288,16 @@
             when(both(next_early, next_same), folded_next.start)
             send_columns()
 
+        @pl.when(plain)
+        def _():
+            meet()
+            send_columns()
+            when(early_east, tell(2, {"lon": east}))
+            when(early_west, tell(3, {"lon": west}))
+            when(below_top, tell(4, {"lat": lat + 1}))
+            when(has_south, *[copy.start for copy in southward])
+            when(has_north, *[copy.start for copy in northward])
+
         @pl.loop(0, levels)
         def _(k):
             z = depth(k.astype(F32))
@@ -315,16 +325,6 @@
         face_y[pl.ds(0, 8)] = pad_n
         face_y[pl.ds(top_row, 8)] = pad_n
 
-        @pl.when(plain)
-        def _():
-            meet()
-            send_columns()
-            when(early_east, tell(2, {"lon": east}))
-            when(early_west, tell(3, {"lon": west}))
-            when(below_top, tell(4, {"lat": lat + 1}))
-            when(has_south, *[copy.start for copy in southward])
-            when(has_north, *[copy.start for copy in northward])
-
         outs = (t_out, s_out)
         loads[4].wait()
         fy[0, pl.ds(rows, 8)] = jnp.zeros((8, 128), F32)
@@ -452,19 +452,19 @@
         eastward.wait_recv()
         westward.wait_recv()
 
-        def joined(own, before, after):
-            left = jnp.where(sl < MID, before, own)
-            right = own if after is None else jnp.where(sl < MID, own, after)
-            a = jnp.where(sl < 4, lanes(left, -1), lanes(right, 4))
-            b = jnp.where(sl < 4, lanes(left, -2), lanes(right, 3))
-            return a, b
-
-        na, nb = joined(px[2 * packs], lanes(from_w[0], -5), lanes(from_e[0], 2))
+        def joined(own, before, after, by_west, by_east):
+            a_west = jnp.where(sl < 2, lanes(before, by_west - 1), lanes(own, -1))
+            a_east = jnp.where(sl < 7, lanes(own, 4), lanes(after, by_east + 4))
+            b_west = jnp.where(sl < 1, lanes(before, by_west - 2), lanes(own, -2))
+            b_east = jnp.where(sl < 6, lanes(own, 3), lanes(after, by_east + 3))
+            return jnp.where(sl < 4, a_west, a_east), jnp.where(sl < 4, b_west, b_east)
+
+        na, nb = joined(px[2 * packs], from_w[0], from_e[0], -5, 2)
         face_n = jnp.minimum(na, nb)
         level_of = packs * (lane // span)
         pairs = [
-            [joined(px[m], from_w[m], from_e[m]) for m in range(packs)],
-            [joined(px[packs + m], lanes(from_w[m], -2), lanes(from_e[m], -2)) for m in range(packs)],
+            [joined(px[m], from_w[m], from_e[m], 0, 0) for m in range(packs)],
+            [joined(px[packs + m], from_w[m], from_e[m], -2, -2) for m in range(packs)],
         ]
         rho_pairs = []
         for m in range(packs):
@@ -489,26 +489,27 @@
             half_scale = jnp.where(jnp.logical_or(level == 0, level == levels - 1), 0.5, 0.25)
             wet = level.astype(F32) < face_n
             keep = jnp.logical_and(wet, used)
-            c = joined(px[2 * packs + 1 + m], lanes(from_w[m], -3), None)[0]
+            u2 = px[2 * packs + 1 + m]
+            c = jnp.where(sl < 4, jnp.where(sl < 2, lanes(from_w[m], -4), lanes(u2, -1)), lanes(u2, 4))
             up, coef = courant_terms(c)
             sk = slope_term(rho_pairs[m][1] - rho_pairs[m][0], zsum_of(sums[2], m), half_scale)
             for i in range(2):
                 qa, qb = pairs[i][m]
                 d = jnp.where(wet, qb - qa, 0.0)
                 f = tracer_flux(keep, c, up, coef, sk, qa, qb, d, lanes(d, 1), lanes(d, -1), zsum_of(sums[i], m))
-                change = f - lanes(f, -1)
-                change = jnp.where(sl < MID, lanes(change, -3), lanes(change, 2))
+                change = jnp.where(sl < MID, lanes(f, -3) - lanes(f, -4), lanes(f, 2) - lanes(f, 1))
                 ex[i, m] = jnp.where(level.astype(F32) < px[2 * packs], change, 0.0)
 
         ends_x = jnp.logical_or(lane < 2, lane > 125)
 
-        for m in range(packs):
-            for i in range(2):
-                packed = ex[i, m]
-                for slot in range(16):
+        packed = [[ex[i, m] for m in range(packs)] for i in range(2)]
+        for slot in range(16):
+            for m in range(packs):
+                for i in range(2):
                     k = packs * (slot // groups) + m
                     at = pl.ds(8 * (slot % groups), 8)
-                    outs[i][k, at] = outs[i][k, at] + jnp.where(ends_x, lanes(packed, -(SLOT * slot + MID)), 0.0)
+                    change = jnp.where(ends_x, lanes(packed[i][m], -(SLOT * slot + MID)), 0.0)
+                    outs[i][k, at] = outs[i][k, at] + change
 
         when(jnp.logical_not(late_west), north_rows)
 

time: 12.9 us -> 12.8 us (level)
  no operation moved by 1% of the time
where the time goes in v6:
time: 12.8 us; the launch traced here: 12.7 us
  Pallas kernels  12 us (94%)
  between operations  0.64 us (5%)
    pallas_call x1, Pallas kernels, body(): pl.pallas_call(make_kernel(nlon, nlat, levels, rows), out_shape=(pltpu.VM...  11.2 us
    pallas_call x1, Pallas kernels, body(): pl.pallas_call(make_edge_kernel(levels, rows), out_shape=(plain, plain),...  0.82 us

profile of v6, /device:TPU:28, one launch (start us, length us, event | category | flops | bytes accessed | tf_op | source)
XLA Modules:
  0.0 12.7 jit_solution(9345684390680269787)
XLA Ops:
  0.6 11.2 %tracer_step.1 = (f32[16,32,128]{2,1,0:T(8,128)S(1)}, f32[16,32,128]{2,1,0:T(8,128)S(1)}, f32[2,16,48,128]{3,2,1,0:T(8,128)S(1)}, f32[16,48,128]{2,1,0:T(8,128)S...) custom-call(f32[16,32,128]{2,1,0:T(8,128)} %t_hbm.1, f32[16,32,128]{2,1,0:T(8,128)} %s_hbm.1, ...), custom_call_target="tpu_custom_call" | custom-call | tf_op jit(solution)/shard_map/tracer_step/pallas_call | solution.py:577
  11.9 0.8 %edge_rows.1 = (f32[16,32,128]{2,1,0:T(8,128)}, f32[16,32,128]{2,1,0:T(8,128)}) custom-call(f32[16,32,128]{2,1,0:T(8,128)S(1)} %get-tuple-element.9.t_part, f32[16,32,128]{2,1,0:T(8,128)S(1)} %get-tuple-element.10.s_part, f32[2,16,48,128]{3,2,1,0:T(8,128)S(1)} %get-tuple-element.11.q, f32[16,48,128]{2,1,0:T(8,128)S(1)} %get-tuple-element.12.v, ...), custom_call_target="tpu_custom_call" | custom-call | tf_op jit(solution)/shard_map/edge_rows/pallas_call | solution.py:620

commit v7 on v6

--- a/solution.py
+++ b/solution.py
@@ -238,8 +238,8 @@
         ]
         folded_next = remote(to_w.at[:, fold_in_group], fb.at[:, hi], 10, {"lon": mirror_next})
         own_next = pltpu.make_async_copy(to_w.at[:, fold_in_group], fb.at[:, hi], load_sem.at[5])
-        eastward = remote(to_e, from_w, 11, {"lon": east})
-        westward = remote(to_w, from_e, 12, {"lon": west})
+        eastward = [remote(to_e.at[m], from_w.at[m], 12 + m, {"lon": east}) for m in range(packs)]
+        westward = remote(to_w, from_e, 11, {"lon": west})
 
         @pl.when(top)
         def _():
@@ -249,8 +249,7 @@
             when(early_east, tell(2, {"lon": east}))
             when(early_west, tell(3, {"lon": west}))
 
-        for load in loads[:4]:
-            load.wait()
+        loads[0].wait()
         packed_n = jnp.zeros((8, 128), F32)
         for slot in range(16):
             part = n[pl.ds(PAD + 8 * (slot % groups), 8)].astype(F32)
@@ -258,8 +257,10 @@
         px[2 * packs] = packed_n
         n_up, n_down = lanes(packed_n, 5), lanes(packed_n, -2)
 
-        @pl.loop(0, packs)
-        def _(m):
+        for load in loads[1:4]:
+            load.wait()
+        top_east = jnp.logical_and(top, jnp.logical_not(late_east))
+        for m in range(packs):
             packed = []
             for field in range(3):
                 one = jnp.zeros((8, 128), F32)
@@ -277,21 +278,21 @@
             s_up = lanes(s2, 2)
             to_e[m] = jnp.where(sl < 3, t2, jnp.where(sl < 5, s_up, jnp.where(sl < 6, lanes(u2, 3), n_up)))
             to_w[m] = jnp.where(sl < 3, n_down, jnp.where(sl < 5, t2, s_up))
+            if m > 0:
+                when(top_east, eastward[m - 1].start)
 
         when(top_self, own_next.start)
-        def send_columns():
-            when(jnp.logical_not(late_east), eastward.start)
+        @pl.when(top)
+        def _():
+            when(both(next_early, next_same), folded_next.start)
+            when(jnp.logical_not(late_east), eastward[-1].start)
             when(jnp.logical_not(late_west), westward.start)
 
-        @pl.when(top)
-        def _():
-            when(both(next_early, next_same), folded_next.start)
-            send_columns()
-
         @pl.when(plain)
         def _():
             meet()
-            send_columns()
+            when(jnp.logical_not(late_east), *[copy.start for copy in eastward])
+            when(jnp.logical_not(late_west), westward.start)
             when(early_east, tell(2, {"lon": east}))
             when(early_west, tell(3, {"lon": west}))
             when(below_top, tell(4, {"lat": lat + 1}))
@@ -382,7 +383,7 @@
         when(top, heard(4), *[copy.start for copy in southward])
         pl.loop(levels // 2, levels)(interior)
 
-        when(late_east, heard(3), eastward.start)
+        when(late_east, heard(3), *[copy.start for copy in eastward])
         when(late_west, heard(2), westward.start)
         when(mirror_late, heard(0), *[copy.start for copy in folded])
         when(next_late, heard(1), folded_next.start)
@@ -449,7 +450,8 @@
 
         when(late_west, north_rows)
 
-        eastward.wait_recv()
+        for copy in eastward:
+            copy.wait_recv()
         westward.wait_recv()
 
         def joined(own, before, after, by_west, by_east):
@@ -513,7 +515,8 @@
 
         when(jnp.logical_not(late_west), north_rows)
 
-        eastward.wait_send()
+        for copy in eastward:
+            copy.wait_send()
         westward.wait_send()
 
         @pl.when(has_south)
@@ -610,8 +613,8 @@
                 pltpu.VMEM((8, cols), I32),
                 pltpu.VMEM((2, packs, 8, cols), F32),
                 pltpu.SemaphoreType.DMA((6,)),
-                pltpu.SemaphoreType.DMA((13,)),
-                pltpu.SemaphoreType.DMA((13,)),
+                pltpu.SemaphoreType.DMA((12 + packs,)),
+                pltpu.SemaphoreType.DMA((12 + packs,)),
                 pltpu.SemaphoreType.REGULAR((5,)),
             ],
             compiler_params=pltpu.CompilerParams(collective_id=0, has_side_effects=True),

time: 12.8 us -> 12.4 us (0.969)
  the two profiles are of different devices: /device:TPU:28 before, /device:TPU:24 now
where the time goes in v7:
time: 12.4 us; the launch traced here: 12.2 us
  Pallas kernels  11.6 us (94%)
  between operations  0.64 us (5%)
    pallas_call x1, Pallas kernels, body(): pl.pallas_call(make_kernel(nlon, nlat, levels, rows), out_shape=(pltpu.VM...  10.8 us
    pallas_call x1, Pallas kernels, body(): pl.pallas_call(make_edge_kernel(levels, rows), out_shape=(plain, plain),...  0.82 us

profile of v7, /device:TPU:24, one launch (start us, length us, event | category | flops | bytes accessed | tf_op | source)
XLA Modules:
  0.0 12.2 jit_solution(11383070057091358306)
XLA Ops:
  0.6 10.8 %tracer_step.1 = (f32[16,32,128]{2,1,0:T(8,128)S(1)}, f32[16,32,128]{2,1,0:T(8,128)S(1)}, f32[2,16,48,128]{3,2,1,0:T(8,128)S(1)}, f32[16,48,128]{2,1,0:T(8,128)S...) custom-call(f32[16,32,128]{2,1,0:T(8,128)} %t_hbm.1, f32[16,32,128]{2,1,0:T(8,128)} %s_hbm.1, ...), custom_call_target="tpu_custom_call" | custom-call | tf_op jit(solution)/shard_map/tracer_step/pallas_call | solution.py:580
  11.4 0.8 %edge_rows.1 = (f32[16,32,128]{2,1,0:T(8,128)}, f32[16,32,128]{2,1,0:T(8,128)}) custom-call(f32[16,32,128]{2,1,0:T(8,128)S(1)} %get-tuple-element.9.t_part, f32[16,32,128]{2,1,0:T(8,128)S(1)} %get-tuple-element.10.s_part, f32[2,16,48,128]{3,2,1,0:T(8,128)S(1)} %get-tuple-element.11.q, f32[16,48,128]{2,1,0:T(8,128)S(1)} %get-tuple-element.12.v, ...), custom_call_target="tpu_custom_call" | custom-call | tf_op jit(solution)/shard_map/edge_rows/pallas_call | solution.py:623

commit v8 on v7

--- a/solution.py
+++ b/solution.py
@@ -130,7 +130,7 @@
         t_hbm, s_hbm, u_hbm, v_hbm, n_hbm,
         t_out, s_out, q, v, n, hp, hn,
         h, hv, hs, h_north, hs_north, rho, u, face_x, keep_x, face_y, keep_y, fy,
-        px, to_e, to_w, from_w, from_e, fa, fb, fan, ex,
+        px, to_e, to_w, from_w, from_e, fa, fb, fan,
         load_sem, send_sem, recv_sem, late_ready,
     ):
         lon = lax.axis_index("lon")
@@ -154,6 +154,11 @@
         late_east = place == quarter - 1
         early_west = place == quarter
         early_east = place == half - 1
+        odd = lax.rem(lat, 2) == 1
+        skew_odd = jnp.logical_and(early_east, jnp.logical_and(odd, plain))
+        skew_even = jnp.logical_and(early_east, jnp.logical_and(jnp.logical_not(odd), plain))
+        level_pair = jnp.logical_not(early_east)
+        prompt = jnp.logical_or(top, jnp.logical_and(skew_even, jnp.logical_not(below_top)))
         mirror_late = jnp.logical_and(top, early)
         mirror_early = jnp.logical_and(top, jnp.logical_not(early))
         next_late = jnp.logical_and(top_far, early)
@@ -174,8 +179,12 @@
         def both(a, b):
             return jnp.logical_or(a, b)
 
-        when(has_south, lambda: greet({"lat": lat - 1}))
-        when(jnp.logical_and(has_north, jnp.logical_not(below_top)), lambda: greet({"lat": lat + 1}))
+        def also(a, b):
+            return jnp.logical_and(a, b)
+
+        when(also(has_south, jnp.logical_not(skew_odd)), lambda: greet({"lat": lat - 1}))
+        northern = jnp.logical_not(both(skew_odd, below_top))
+        when(also(has_north, northern), lambda: greet({"lat": lat + 1}))
         when(mirror_late, lambda: greet({"lon": mirror}))
         when(both(next_late, next_same), lambda: greet({"lon": mirror_next}))
         when(jnp.logical_not(early_east), lambda: greet({"lon": east}))
@@ -198,7 +207,7 @@
         sl = lane % SLOT
 
         greetings = (
-            jnp.logical_and(has_south, plain), has_north, mirror_early, both(next_early, next_same),
+            also(has_south, both(skew_odd, also(level_pair, plain))), also(has_north, both(both(skew_odd, below_top), level_pair)), mirror_early, both(next_early, next_same),
             jnp.logical_not(late_west), jnp.logical_not(late_east),
         )
 
@@ -241,13 +250,17 @@
         eastward = [remote(to_e.at[m], from_w.at[m], 12 + m, {"lon": east}) for m in range(packs)]
         westward = remote(to_w, from_e, 11, {"lon": west})
 
-        @pl.when(top)
+        def tell_even():
+            when(also(skew_odd, has_north), tell(5, {"lat": lat + 1}))
+            when(also(skew_odd, has_south), tell(6, {"lat": lat - 1}))
+
+        @pl.when(prompt)
         def _():
             meet()
             when(mirror_early, *[copy.start for copy in folded], tell(0, {"lon": mirror}))
             when(next_early, tell(1, {"lon": mirror_next}))
             when(early_east, tell(2, {"lon": east}))
-            when(early_west, tell(3, {"lon": west}))
+            when(also(top, early_west), tell(3, {"lon": west}))
 
         loads[0].wait()
         packed_n = jnp.zeros((8, 128), F32)
@@ -259,7 +272,7 @@
 
         for load in loads[1:4]:
             load.wait()
-        top_east = jnp.logical_and(top, jnp.logical_not(late_east))
+        prompt_east = also(prompt, jnp.logical_not(late_east))
         for m in range(packs):
             packed = []
             for field in range(3):
@@ -279,24 +292,25 @@
             to_e[m] = jnp.where(sl < 3, t2, jnp.where(sl < 5, s_up, jnp.where(sl < 6, lanes(u2, 3), n_up)))
             to_w[m] = jnp.where(sl < 3, n_down, jnp.where(sl < 5, t2, s_up))
             if m > 0:
-                when(top_east, eastward[m - 1].start)
+                when(prompt_east, eastward[m - 1].start)
 
         when(top_self, own_next.start)
-        @pl.when(top)
+        @pl.when(prompt)
         def _():
             when(both(next_early, next_same), folded_next.start)
             when(jnp.logical_not(late_east), eastward[-1].start)
             when(jnp.logical_not(late_west), westward.start)
 
-        @pl.when(plain)
+        @pl.when(jnp.logical_not(prompt))
         def _():
             meet()
             when(jnp.logical_not(late_east), *[copy.start for copy in eastward])
             when(jnp.logical_not(late_west), westward.start)
             when(early_east, tell(2, {"lon": east}))
             when(early_west, tell(3, {"lon": west}))
+            tell_even()
             when(below_top, tell(4, {"lat": lat + 1}))
-            when(has_south, *[copy.start for copy in southward])
+            when(also(has_south, jnp.logical_not(skew_even)), *[copy.start for copy in southward])
             when(has_north, *[copy.start for copy in northward])
 
         @pl.loop(0, levels)
@@ -383,6 +397,8 @@
         when(top, heard(4), *[copy.start for copy in southward])
         pl.loop(levels // 2, levels)(interior)
 
+        when(also(skew_even, has_south), heard(5), *[copy.start for copy in southward])
+        when(also(skew_even, jnp.logical_not(below_top)), heard(6), *[copy.start for copy in northward])
         when(late_east, heard(3), *[copy.start for copy in eastward])
         when(late_west, heard(2), westward.start)
         when(mirror_late, heard(0), *[copy.start for copy in folded])
@@ -486,6 +502,7 @@
             return above - below
 
         used = jnp.logical_or(jnp.logical_or(sl == 1, sl == 2), jnp.logical_or(sl == 5, sl == 6))
+        changes = [[], []]
         for m in range(packs):
             level = level_of + m
             half_scale = jnp.where(jnp.logical_or(level == 0, level == levels - 1), 0.5, 0.25)
@@ -500,17 +517,16 @@
                 d = jnp.where(wet, qb - qa, 0.0)
                 f = tracer_flux(keep, c, up, coef, sk, qa, qb, d, lanes(d, 1), lanes(d, -1), zsum_of(sums[i], m))
                 change = jnp.where(sl < MID, lanes(f, -3) - lanes(f, -4), lanes(f, 2) - lanes(f, 1))
-                ex[i, m] = jnp.where(level.astype(F32) < px[2 * packs], change, 0.0)
+                changes[i].append(jnp.where(level.astype(F32) < px[2 * packs], change, 0.0))
 
         ends_x = jnp.logical_or(lane < 2, lane > 125)
 
-        packed = [[ex[i, m] for m in range(packs)] for i in range(2)]
         for slot in range(16):
             for m in range(packs):
                 for i in range(2):
                     k = packs * (slot // groups) + m
                     at = pl.ds(8 * (slot % groups), 8)
-                    change = jnp.where(ends_x, lanes(packed[i][m], -(SLOT * slot + MID)), 0.0)
+                    change = jnp.where(ends_x, lanes(changes[i][m], -(SLOT * slot + MID)), 0.0)
                     outs[i][k, at] = outs[i][k, at] + change
 
         when(jnp.logical_not(late_west), north_rows)
@@ -611,11 +627,10 @@
                 pltpu.VMEM((2, levels, 8, cols), F32),
                 pltpu.VMEM((packs, 8, cols), F32),
                 pltpu.VMEM((8, cols), I32),
-                pltpu.VMEM((2, packs, 8, cols), F32),
                 pltpu.SemaphoreType.DMA((6,)),
                 pltpu.SemaphoreType.DMA((12 + packs,)),
                 pltpu.SemaphoreType.DMA((12 + packs,)),
-                pltpu.SemaphoreType.REGULAR((5,)),
+                pltpu.SemaphoreType.REGULAR((7,)),
             ],
             compiler_params=pltpu.CompilerParams(collective_id=0, has_side_effects=True),
             name="tracer_step",

time: 12.4 us -> 12.2 us (0.984)
  the two profiles are of different devices: /device:TPU:24 before, /device:TPU:4 now
where the time goes in v8:
time: 12.2 us; the launch traced here: 12.1 us
  Pallas kernels  11.4 us (93%)
  between operations  0.64 us (5%)
    pallas_call x1, Pallas kernels, body(): pl.pallas_call(make_kernel(nlon, nlat, levels, rows), out_shape=(pltpu.VM...  10.6 us
    pallas_call x1, Pallas kernels, body(): pl.pallas_call(make_edge_kernel(levels, rows), out_shape=(plain, plain),...  0.82 us

profile of v8, /device:TPU:4, one launch (start us, length us, event | category | flops | bytes accessed | tf_op | source)
XLA Modules:
  0.0 12.1 jit_solution(4951793836515550754)
XLA Ops:
  0.6 10.6 %tracer_step.1 = (f32[16,32,128]{2,1,0:T(8,128)S(1)}, f32[16,32,128]{2,1,0:T(8,128)S(1)}, f32[2,16,48,128]{3,2,1,0:T(8,128)S(1)}, f32[16,48,128]{2,1,0:T(8,128)S...) custom-call(f32[16,32,128]{2,1,0:T(8,128)} %t_hbm.1, f32[16,32,128]{2,1,0:T(8,128)} %s_hbm.1, ...), custom_call_target="tpu_custom_call" | custom-call | tf_op jit(solution)/shard_map/tracer_step/pallas_call | solution.py:596
  11.2 0.8 %edge_rows.1 = (f32[16,32,128]{2,1,0:T(8,128)}, f32[16,32,128]{2,1,0:T(8,128)}) custom-call(f32[16,32,128]{2,1,0:T(8,128)S(1)} %get-tuple-element.9.t_part, f32[16,32,128]{2,1,0:T(8,128)S(1)} %get-tuple-element.10.s_part, f32[2,16,48,128]{3,2,1,0:T(8,128)S(1)} %get-tuple-element.11.q, f32[16,48,128]{2,1,0:T(8,128)S(1)} %get-tuple-element.12.v, ...), custom_call_target="tpu_custom_call" | custom-call | tf_op jit(solution)/shard_map/edge_rows/pallas_call | solution.py:638

commit v9 on v8

--- a/solution.py
+++ b/solution.py
@@ -227,6 +227,7 @@
 
         first, last = pl.ds(0, 2), pl.ds(rows - 2, 2)
         fold = pl.ds(rows - 3, 2)
+        lower, upper = pl.ds(0, levels // 2), pl.ds(levels // 2, levels // 2)
         fold_in_group = pl.ds(5, 2)
         lo, hi = pl.ds(0, 2), pl.ds(6, 2)
         northward = [
@@ -241,9 +242,11 @@
             remote(n_hbm.at[first], hs_north.at[hi], 6, {"lat": lat - 1}),
         ]
         folded = [
-            remote(t_hbm.at[:, fold], fa.at[0, :, hi], 7, {"lon": mirror}),
-            remote(s_hbm.at[:, fold], fa.at[1, :, hi], 8, {"lon": mirror}),
             remote(n_hbm.at[fold], fan.at[hi], 9, {"lon": mirror}),
+            remote(t_hbm.at[lower, fold], fa.at[0, lower, hi], 7, {"lon": mirror}),
+            remote(s_hbm.at[lower, fold], fa.at[1, lower, hi], 8, {"lon": mirror}),
+            remote(t_hbm.at[upper, fold], fa.at[0, upper, hi], 12 + packs, {"lon": mirror}),
+            remote(s_hbm.at[upper, fold], fa.at[1, upper, hi], 13 + packs, {"lon": mirror}),
         ]
         folded_next = remote(to_w.at[:, fold_in_group], fb.at[:, hi], 10, {"lon": mirror_next})
         own_next = pltpu.make_async_copy(to_w.at[:, fold_in_group], fb.at[:, hi], load_sem.at[5])
@@ -628,8 +631,8 @@
                 pltpu.VMEM((packs, 8, cols), F32),
                 pltpu.VMEM((8, cols), I32),
                 pltpu.SemaphoreType.DMA((6,)),
-                pltpu.SemaphoreType.DMA((12 + packs,)),
-                pltpu.SemaphoreType.DMA((12 + packs,)),
+                pltpu.SemaphoreType.DMA((14 + packs,)),
+                pltpu.SemaphoreType.DMA((14 + packs,)),
                 pltpu.SemaphoreType.REGULAR((7,)),
             ],
             compiler_params=pltpu.CompilerParams(collective_id=0, has_side_effects=True),

time: 12.2 us -> 12.3 us (level)
  no operation moved by 1% of the time
where the time goes in v9:
time: 12.3 us; the launch traced here: 12.1 us
  Pallas kernels  11.5 us (93%)
  between operations  0.64 us (5%)
    pallas_call x1, Pallas kernels, body(): pl.pallas_call(make_kernel(nlon, nlat, levels, rows), out_shape=(pltpu.VM...  10.6 us
    pallas_call x1, Pallas kernels, body(): pl.pallas_call(make_edge_kernel(levels, rows), out_shape=(plain, plain),...  0.82 us

profile of v9, /device:TPU:4, one launch (start us, length us, event | category | flops | bytes accessed | tf_op | source)
XLA Modules:
  0.0 12.1 jit_solution(9278920595950527705)
XLA Ops:
  0.6 10.6 %tracer_step.1 = (f32[16,32,128]{2,1,0:T(8,128)S(1)}, f32[16,32,128]{2,1,0:T(8,128)S(1)}, f32[2,16,48,128]{3,2,1,0:T(8,128)S(1)}, f32[16,48,128]{2,1,0:T(8,128)S...) custom-call(f32[16,32,128]{2,1,0:T(8,128)} %t_hbm.1, f32[16,32,128]{2,1,0:T(8,128)} %s_hbm.1, ...), custom_call_target="tpu_custom_call" | custom-call | tf_op jit(solution)/shard_map/tracer_step/pallas_call | solution.py:599
  11.3 0.8 %edge_rows.1 = (f32[16,32,128]{2,1,0:T(8,128)}, f32[16,32,128]{2,1,0:T(8,128)}) custom-call(f32[16,32,128]{2,1,0:T(8,128)S(1)} %get-tuple-element.9.t_part, f32[16,32,128]{2,1,0:T(8,128)S(1)} %get-tuple-element.10.s_part, f32[2,16,48,128]{3,2,1,0:T(8,128)S(1)} %get-tuple-element.11.q, f32[16,48,128]{2,1,0:T(8,128)S(1)} %get-tuple-element.12.v, ...), custom_call_target="tpu_custom_call" | custom-call | tf_op jit(solution)/shard_map/edge_rows/pallas_call | solution.py:641

commit v10 on v8

--- a/solution.py
+++ b/solution.py
@@ -182,14 +182,6 @@
         def also(a, b):
             return jnp.logical_and(a, b)
 
-        when(also(has_south, jnp.logical_not(skew_odd)), lambda: greet({"lat": lat - 1}))
-        northern = jnp.logical_not(both(skew_odd, below_top))
-        when(also(has_north, northern), lambda: greet({"lat": lat + 1}))
-        when(mirror_late, lambda: greet({"lon": mirror}))
-        when(both(next_late, next_same), lambda: greet({"lon": mirror_next}))
-        when(jnp.logical_not(early_east), lambda: greet({"lon": east}))
-        when(jnp.logical_not(early_west), lambda: greet({"lon": west}))
-
         body_rows = pl.ds(PAD, rows)
         loads = [
             pltpu.make_async_copy(n_hbm, n.at[body_rows], load_sem.at[0]),
@@ -198,8 +190,18 @@
             pltpu.make_async_copy(u_hbm, u, load_sem.at[3]),
             pltpu.make_async_copy(v_hbm, v.at[:, body_rows], load_sem.at[4]),
         ]
-        for load in loads:
+        for load in loads[:4]:
             load.start()
+
+        when(also(has_south, jnp.logical_not(skew_odd)), lambda: greet({"lat": lat - 1}))
+        northern = jnp.logical_not(both(skew_odd, below_top))
+        when(also(has_north, northern), lambda: greet({"lat": lat + 1}))
+        when(mirror_late, lambda: greet({"lon": mirror}))
+        when(both(next_late, next_same), lambda: greet({"lon": mirror_next}))
+        when(jnp.logical_not(early_east), lambda: greet({"lon": east}))
+        when(jnp.logical_not(early_west), lambda: greet({"lon": west}))
+
+        loads[4].start()
 
         lane = lax.broadcasted_iota(I32, (8, 128), 1)
         row = lax.broadcasted_iota(I32, (8, 128), 0)

time: 12.2 us -> 12.2 us (level)
  no operation moved by 1% of the time
where the time goes in v10:
time: 12.2 us; the launch traced here: 12.1 us
  Pallas kernels  11.4 us (93%)
  between operations  0.64 us (5%)
    pallas_call x1, Pallas kernels, body(): pl.pallas_call(make_kernel(nlon, nlat, levels, rows), out_shape=(pltpu.VM...  10.6 us
    pallas_call x1, Pallas kernels, body(): pl.pallas_call(make_edge_kernel(levels, rows), out_shape=(plain, plain),...  0.82 us

profile of v10, /device:TPU:4, one launch (start us, length us, event | category | flops | bytes accessed | tf_op | source)
XLA Modules:
  0.0 12.1 jit_solution(14600788798170683248)
XLA Ops:
  0.6 10.6 %tracer_step.1 = (f32[16,32,128]{2,1,0:T(8,128)S(1)}, f32[16,32,128]{2,1,0:T(8,128)S(1)}, f32[2,16,48,128]{3,2,1,0:T(8,128)S(1)}, f32[16,48,128]{2,1,0:T(8,128)S...) custom-call(f32[16,32,128]{2,1,0:T(8,128)} %t_hbm.1, f32[16,32,128]{2,1,0:T(8,128)} %s_hbm.1, ...), custom_call_target="tpu_custom_call" | custom-call | tf_op jit(solution)/shard_map/tracer_step/pallas_call | solution.py:598
  11.2 0.8 %edge_rows.1 = (f32[16,32,128]{2,1,0:T(8,128)}, f32[16,32,128]{2,1,0:T(8,128)}) custom-call(f32[16,32,128]{2,1,0:T(8,128)S(1)} %get-tuple-element.9.t_part, f32[16,32,128]{2,1,0:T(8,128)S(1)} %get-tuple-element.10.s_part, f32[2,16,48,128]{3,2,1,0:T(8,128)S(1)} %get-tuple-element.11.q, f32[16,48,128]{2,1,0:T(8,128)S(1)} %get-tuple-element.12.v, ...), custom_call_target="tpu_custom_call" | custom-call | tf_op jit(solution)/shard_map/edge_rows/pallas_call | solution.py:640
